TPU v7x, 256 devices: a whole 4x4x8 slice. The times are simulated.
256 devices in a mesh: ctx: 32 (over x, z), tp: 8 (over y, core).
Axes of the slice: x: 4, y: 4, z: 8, core: 2. Of those that a mesh axis runs over, the one named last changes fastest.
Arguments:
- tokens: int32 [8192], P('ctx'), may hold values from 0 to 3
- rc_map: int32 [4], replicated, may hold values from 0 to 3, each once
- embedding: bfloat16 [4, 2048], replicated, may hold values from -6 to 6
- norm_gain: float32 [2048], replicated, may hold values from 0.5 to 1.5
- w_values: bfloat16 [2048, 4096], P(None, 'tp'), may hold values from -0.125 to 0.125
- w_gates: bfloat16 [2048, 4096], P(None, 'tp'), may hold values from -0.125 to 0.125
- w_states: bfloat16 [2048, 256], replicated, may hold values from -0.125 to 0.125
- w_steps: bfloat16 [2048, 32], P(None, 'tp'), may hold values from -0.125 to 0.125
- conv_values: float32 [4, 4096], P(None, 'tp'), may hold values from -0.5 to 0.5
- conv_states: float32 [4, 256], replicated, may hold values from -0.5 to 0.5
- step_bias: float32 [32], P('tp'), may hold values from -1 to 1
- log_rate: float32 [32], P('tp'), as said below
- skip_gain: float32 [32], P('tp'), may hold values from 0.5 to 1.5
- head_gain: float32 [4096], P('tp'), may hold values from 0.5 to 1.5
- cotangent: bfloat16 [8192, 4096], P('ctx', 'tp'), may hold values from -6 to 6
Outputs:
- encoded: bfloat16 [8192, 4096], P('ctx', 'tp')
- grad_log_rate: float32 [32], replicated
- grad_step_bias: float32 [32], replicated
- grad_conv_states: float32 [4, 256], replicated
Inputs may be any that keep to these rules, and one draw needn't show every extreme that they name: `rc_map`: a permutation of the four ids. exp(log_rate) lies between 0.3 / 8192 and 0.1.
All inputs are finite; a program needn't handle non-finite values.
Results may differ from a plain program's by a relative error of at most 0.001.
The roundings to bfloat16 on the way count: a program that leaves them out, or rounds other values in their place, can miss the bound.
Values sent between devices are 32-bit elements; how exact they have to be, the bound alone decides.
A program may use at most 128 MiB of HBM per device.

v0:
```python
import math

import jax
import jax.numpy as jnp
from jax import lax
from jax.experimental import pallas as pl
from jax.experimental.pallas import tpu as pltpu
from jax.sharding import PartitionSpec as P

F32 = jnp.float32
BF16 = jnp.bfloat16
HEAD = 128
CONV = 4
EPS = 1e-05
MESH = pl.DeviceIdType.MESH
VM = pl.BlockSpec(memory_space=pltpu.VMEM)
SM = pl.BlockSpec(memory_space=pltpu.SMEM)


def split(v):
    hi = v.astype(BF16)
    return hi, (v - hi.astype(F32)).astype(BF16)


def dot(a, b, ca=1, cb=0):
    return lax.dot_general(a, b, (((ca,), (cb,)), ((), ())), preferred_element_type=F32)


def mm(a, b, ca=1, cb=0):
    return dot(a[0], b[0], ca, cb) + (dot(a[0], b[1], ca, cb) + dot(a[1], b[0], ca, cb))


def iota(shape, dim):
    return lax.broadcasted_iota(jnp.int32, shape, dim)


def back_one(v, fill):
    rolled = pltpu.roll(v, 1, 1)
    wrapped = pltpu.roll(rolled, 1, 0)
    moved = jnp.where(iota(v.shape, 1) == 0, wrapped, rolled)
    first = (iota(v.shape, 0) == 0) & (iota(v.shape, 1) == 0)
    return jnp.where(first, fill, moved)


def ahead_one(v, fill):
    rows, lanes = v.shape
    rolled = pltpu.roll(v, lanes - 1, 1)
    wrapped = pltpu.roll(rolled, rows - 1, 0)
    moved = jnp.where(iota(v.shape, 1) == lanes - 1, wrapped, rolled)
    last = (iota(v.shape, 0) == rows - 1) & (iota(v.shape, 1) == lanes - 1)
    return jnp.where(last, fill, moved)


def softplus(v):
    return jnp.maximum(v, 0.0) + jnp.log1p(jnp.exp(-jnp.abs(v)))


def mixer_kernel(
    place, rc, bias, log_rate, skip, tok_ref, emb_ref, ng_ref, wv_ref, wg_ref, ws_ref, wst_ref,
    cv_ref, cs_ref, hg_ref, cot_ref, enc_ref, pay_ref, fwd_ref, rev_ref, kmer_ref, rows_ref,
    *, loss_scale,
):
    me, slot = place()
    chunks = tok_ref.shape[0]
    blocks = chunks // 2
    inner = cv_ref.shape[1]
    heads = inner // HEAD
    own = cot_ref.shape[0]

    e = emb_ref[...].astype(F32)
    scale = lax.rsqrt(jnp.mean(e * e, axis=1, keepdims=True) + EPS)
    normed = (e * scale * ng_ref[...]).astype(BF16)
    normed = jnp.concatenate([normed, jnp.zeros((12, e.shape[1]), BF16)], axis=0)
    table_v = dot(normed, wv_ref[...])[0:4]
    table_s = dot(normed, ws_ref[...])[0:4]
    table_z = dot(normed, wg_ref[...])[0:4]
    table_d = dot(normed, wst_ref[...])[0:4]
    lane_h = iota((1, heads), 1)
    bias_row = jnp.zeros((1, heads), F32)
    rate_row = jnp.zeros((1, heads), F32)
    for h in range(heads):
        bias_row = jnp.where(lane_h == h, bias[h], bias_row)
        rate_row = jnp.where(lane_h == h, log_rate[h], rate_row)
    rate_row = jnp.exp(rate_row)
    pre_step = table_d + bias_row
    step_t = softplus(pre_step)
    sig_t = 1.0 / (1.0 + jnp.exp(-pre_step))
    gate_t = table_z / (1.0 + jnp.exp(-table_z))
    table_vs = jnp.concatenate([table_v, table_s], axis=1)
    taps = jnp.concatenate([cv_ref[...], cs_ref[...]], axis=1)
    tail = jnp.concatenate(
        [gate_t, step_t, sig_t, jnp.zeros((4, 128 - 2 * heads), F32)], axis=1
    )
    parts = []
    for k in range(CONV):
        rest = tail if k == CONV - 1 else jnp.zeros_like(tail)
        parts.append(jnp.concatenate([table_vs * taps[k : k + 1], rest], axis=1))
    per_tap = jnp.concatenate(parts, axis=0)
    p_hi = per_tap.astype(BF16)
    p_rest = per_tap - p_hi.astype(F32)
    p_mid = p_rest.astype(BF16)
    p_low = (p_rest - p_mid.astype(F32)).astype(BF16)
    per_tap3 = jnp.concatenate([p_hi, p_mid, p_low], axis=0)

    tok = tok_ref[...].astype(F32)
    comp = jnp.zeros_like(tok)
    for a in range(4):
        comp = jnp.where(tok == a, rc[a].astype(F32), comp)
    f_shift, r_shift = [tok], [comp]
    for _ in range(CONV - 1):
        f_shift.append(back_one(f_shift[-1], -1.0))
        r_shift.append(ahead_one(r_shift[-1], -1.0))
    for d in range(CONV):
        fwd_ref[d] = f_shift[d]
        rev_ref[d] = r_shift[d]

    row = iota(tok.shape, 0)
    position = row * 128 + iota(tok.shape, 1)
    before = row < 2 * me
    outside = before | (row >= 2 * me + 2)
    kmer_f = f_shift[0] + 4.0 * f_shift[1] + 16.0 * f_shift[2] + 64.0 * f_shift[3]
    kmer_r = r_shift[0] + 4.0 * r_shift[1] + 16.0 * r_shift[2] + 64.0 * r_shift[3]
    kmer = jnp.where(before, kmer_f, kmer_r)
    edge = (before & (position < CONV - 1)) | (position >= chunks * 128 - (CONV - 1))
    kmer_ref[...] = jnp.where(edge & outside, -1.0, kmer)
    mixed = jnp.where(outside, jnp.where(before, tok, comp), -1.0)
    tri = (iota((128, 128), 0) <= iota((128, 128), 1)).astype(BF16)
    ones = jnp.ones((128, 128), BF16)
    strict = (iota((chunks, chunks), 1) < iota((chunks, chunks), 0)).astype(BF16)
    counts = []
    for a in range(4):
        hit = (mixed == a).astype(F32)
        hit16 = hit.astype(BF16)
        within = dot(hit16, tri)
        offset = dot(strict, dot(hit16, ones).astype(BF16))
        total_f = jnp.sum(jnp.where(before, hit, 0.0), keepdims=True)
        inclusive = within + offset - total_f
        counts.append(jnp.where(before, -inclusive, inclusive - hit))
    for h in range(heads):
        steps_sum = sum(counts[a] * step_t[a : a + 1, h : h + 1] for a in range(4))
        sig_sum = sum(counts[a] * sig_t[a : a + 1, h : h + 1] for a in range(4))
        exponent = -(rate_row[:, h : h + 1] * steps_sum)
        decay = jnp.where(outside, jnp.exp(exponent), 0.0)
        for q, value in enumerate((decay, decay * exponent, decay * sig_sum)):
            base = (q * heads + h) * chunks
            rows_ref[base : base + chunks, :] = value
    for q in range(3 * heads, 16):
        rows_ref[q * chunks : (q + 1) * chunks, :] = jnp.zeros((chunks, 128), F32)

    kmer_id = iota((256, 128), 0).astype(F32)

    def load_rows(chunk):
        return rows_ref[pl.ds(chunk, 16, stride=chunks), :]

    def one_hot(chunk):
        return (jnp.broadcast_to(kmer_ref[pl.ds(chunk, 1), :], (256, 128)) == kmer_id).astype(F32)

    def add_block(i, acc):
        weights = jnp.concatenate([load_rows(2 * i), load_rows(2 * i + 1)], axis=1)
        w_f = split(jnp.where(i < me, weights, 0.0))
        w_r = split(jnp.where(i > me, weights, 0.0))
        stacked = jnp.concatenate([w_f[0], w_f[1], w_r[0], w_r[1]], axis=0)
        hits = jnp.concatenate([one_hot(2 * i), one_hot(2 * i + 1)], axis=1).astype(BF16)
        return acc + dot(hits, stacked, 1, 1)

    acc = lax.fori_loop(0, blocks, add_block, jnp.zeros((256, 64), F32), unroll=4)
    lane = iota((16, 128), 1)
    e_f = split(jnp.where(lane < CONV - 1, load_rows(0), 0.0))
    e_r = split(jnp.where(lane >= 128 - (CONV - 1), load_rows(chunks - 1), 0.0))
    edge_rows = jnp.concatenate(
        [e_f[0], e_f[1], e_r[0], e_r[1]], axis=0
    )
    pick_row = iota((16, 128), 0)
    pick = (lane == jnp.where(pick_row < 8, pick_row, pick_row + 112)).astype(BF16)
    acc = jnp.concatenate([acc, dot(pick, edge_rows, 1, 1)], axis=0)
    sources_f = acc[:, 0:16] + acc[:, 16:32]
    sources_r = acc[:, 32:48] + acc[:, 48:64]

    def local_row(ref, d):
        pair = ref[d, pl.ds(2 * me, 2), :]
        return jnp.concatenate([pair[0:1], pair[1:2]], axis=1)

    hits_t = []
    for k in range(CONV):
        d = CONV - 1 - k
        lanes1 = iota((1, 128), 1)
        ends = jnp.where(
            lanes1 < 64, fwd_ref[d, 0:1, :], rev_ref[d, chunks - 1 : chunks, :]
        )
        line = jnp.concatenate([local_row(fwd_ref, d), local_row(rev_ref, d), ends], axis=1)
        hits_t.append(
            (jnp.broadcast_to(line, (4, line.shape[1])) == iota((4, line.shape[1]), 0).astype(F32))
        )
    hits_t = jnp.concatenate([h.astype(F32) for h in hits_t], axis=0)
    hits3_t = jnp.concatenate([hits_t, hits_t, hits_t], axis=0).astype(BF16)
    local_sum = dot(hits3_t, per_tap3, 0, 0)
    column = iota((256, 48), 1) % 16
    digit = lax.shift_right_logical(iota((256, 48), 0), 2 * (3 - column // 4)) & 3
    kmer_hits = (digit == column % 4).astype(F32).astype(BF16)
    kmer_sum = dot(kmer_hits, per_tap3)
    ends_sum = jnp.concatenate([local_sum[512:520], local_sum[632:640]], axis=0)
    kmer_sum = jnp.concatenate([kmer_sum, ends_sum], axis=0)

    def silu(v):
        return v / (1.0 + jnp.exp(-v))

    def silu_slope(v):
        s = 1.0 / (1.0 + jnp.exp(-v))
        return s + v * s * (1.0 - s)

    width = inner + 2 * HEAD
    kx = silu(kmer_sum[:, :inner])
    kb = silu(kmer_sum[:, inner : inner + HEAD])
    k_steps = kmer_sum[:, width + inner : width + inner + 128]
    kx_s = [split(kx[:, h * HEAD : (h + 1) * HEAD]) for h in range(heads)]
    kb_s = split(kb)

    tri_in = (iota((own, own), 0) <= iota((own, own), 1)).astype(BF16)
    tri_out = (iota((own, own), 0) >= iota((own, own), 1)).astype(BF16)
    pad4 = jnp.zeros((12, own), BF16)
    hits_f = hits_t[12:16, 0:own].astype(BF16)
    hits_r = hits_t[12:16, own : 2 * own].astype(BF16)
    n_f = dot(jnp.concatenate([hits_f, pad4], axis=0), tri_in)
    n_r = dot(jnp.concatenate([hits_r, pad4], axis=0), tri_out)
    cum_rows, sig_rows, step_rows, own_sig = [], [], [], []
    for counted, hit in ((n_f, hits_t[12:16, 0:own]), (n_r, hits_t[12:16, own : 2 * own])):
        for h in range(heads):
            steps_sum = sum(counted[a : a + 1] * step_t[a : a + 1, h : h + 1] for a in range(4))
            cum_rows.append(-(rate_row[:, h : h + 1] * steps_sum))
            sig_rows.append(
                sum(counted[a : a + 1] * sig_t[a : a + 1, h : h + 1] for a in range(4))
            )
            step_rows.append(sum(hit[a : a + 1] * step_t[a : a + 1, h : h + 1] for a in range(4)))
            own_sig.append(sum(hit[a : a + 1] * sig_t[a : a + 1, h : h + 1] for a in range(4)))
    stack = jnp.concatenate(
        cum_rows + sig_rows + [jnp.zeros((128 - 4 * heads, own), F32)], axis=0
    )
    columns = jnp.transpose(stack)

    cot = cot_ref[...].astype(F32) * loss_scale
    gain = hg_ref[...]
    encoded = jnp.zeros((own, inner), F32)
    d_kb = jnp.zeros(kb.shape, F32)
    rate_grads = [jnp.zeros((1, 1), F32)] * heads
    bias_grads = [jnp.zeros((1, 1), F32)] * heads
    tap_sums = jnp.zeros((16, 2 * HEAD), F32)

    def total(v):
        return jnp.sum(v, keepdims=True)

    for strand in range(2):
        summed = local_sum[strand * own : (strand + 1) * own]
        sources = (sources_f, sources_r)[strand]
        x = silu(summed[:, :inner])
        states = silu(summed[:, inner:width])
        gates = summed[:, width : width + inner]
        b_s = split(states[:, :HEAD])
        c = states[:, HEAD:]
        c_s = split(c)
        scores = mm(c_s, b_s, 1, 1)
        if strand == 0:
            causal = iota((own, own), 0) >= iota((own, own), 1)
        else:
            causal = iota((own, own), 0) <= iota((own, own), 1)
        d_scores = jnp.zeros((own, own), F32)
        d_c = jnp.zeros((own, HEAD), F32)
        for h in range(heads):
            n = strand * heads + h
            part = slice(h * HEAD, (h + 1) * HEAD)
            w0 = k_steps[:, h : h + 1] * sources[:, h : h + 1]
            w1 = k_steps[:, h : h + 1] * sources[:, heads + h : heads + h + 1]
            rate = rate_row[:, h : h + 1]
            w2 = (
                k_steps[:, heads + h : heads + h + 1] * sources[:, h : h + 1]
                - rate * k_steps[:, h : h + 1] * sources[:, 2 * heads + h : 2 * heads + h + 1]
            )
            start_s = split(mm(kb_s, split(kx[:, part] * w0), 0, 0))
            cum_c = columns[:, n : n + 1]
            sig_c = columns[:, 2 * heads + n : 2 * heads + n + 1]
            cum_r, sig_r, step_r = cum_rows[n], sig_rows[n], step_rows[n]
            decays = jnp.where(causal, jnp.exp(cum_c - cum_r), 0.0) * step_r
            x_h = x[:, part]
            x_s = split(x_h)
            grow = jnp.exp(cum_c)
            from_start = grow * mm(c_s, start_s)
            y = mm(split(scores * decays), x_s) + from_start + skip[h] * x_h
            gate = gates[:, part]
            gated = y * gate
            inv = lax.rsqrt(jnp.mean(gated * gated, axis=1, keepdims=True) + EPS)
            normal = gated * inv
            out = normal * gain[:, part]
            enc_part = encoded[:, part] + out
            if strand == 0:
                rows_ref[h * own : (h + 1) * own, :] = out
            else:
                enc_ref[:, part] = (rows_ref[h * own : (h + 1) * own, :] + out).astype(BF16)
            d_normal = cot[:, part] * gain[:, part]
            d_y = inv * (d_normal - normal * jnp.mean(normal * d_normal, axis=1, keepdims=True))
            d_y = d_y * gate
            d_y_s = split(d_y)
            mixed_grad = mm(d_y_s, x_s, 1, 1) * decays
            d_scores = d_scores + mixed_grad
            weighted = mixed_grad * scores
            row_sum = jnp.sum(weighted, axis=1, keepdims=True) + jnp.sum(
                d_y * from_start, axis=1, keepdims=True
            )
            col_sum = jnp.sum(weighted, axis=0, keepdims=True)
            grown_s = split(d_y * grow)
            d_c = d_c + mm(grown_s, start_s, 1, 1)
            d_start_s = split(mm(c_s, grown_s, 0, 0))
            pulled = mm(kx_s[h], d_start_s, 1, 1)
            d_kb = d_kb + pulled * w0
            d_w0 = jnp.sum(pulled * kb, axis=1, keepdims=True)
            rate_grads[h] = (
                rate_grads[h] + total(row_sum * cum_c) - total(col_sum * cum_r) + total(d_w0 * w1)
            )
            bias_grads[h] = (
                bias_grads[h]
                + rate * (total(col_sum * sig_r) - total(row_sum * sig_c))
                + total(jnp.where(step_r > 0.0, col_sum * own_sig[n] / step_r, 0.0))
                + total(d_w0 * w2)
            )
        d_scores_s = split(d_scores)
        d_c = d_c + mm(d_scores_s, b_s)
        d_b = mm(d_scores_s, c_s, 0, 0)
        d_sum = jnp.concatenate([d_b, d_c], axis=1) * silu_slope(summed[:, inner:width])
        d_sum_s = split(d_sum)
        hits = hits_t[:, strand * own : (strand + 1) * own].astype(BF16)
        tap_sums = tap_sums + dot(hits, d_sum_s[0]) + dot(hits, d_sum_s[1])
    d_kb = d_kb * silu_slope(kmer_sum[:, inner : inner + HEAD])
    d_kb_s = split(d_kb)
    end_hits = hits_t[:, 2 * own : 2 * own + 128]
    pick_s = pick
    b_sums = dot(kmer_hits[:, 0:16], d_kb_s[0][0:256], 0, 0) + dot(
        kmer_hits[:, 0:16], d_kb_s[1][0:256], 0, 0
    )
    end_pick = dot(end_hits.astype(BF16), pick_s, 1, 1).astype(BF16)
    b_sums = b_sums + dot(end_pick, d_kb_s[0][256:272]) + dot(end_pick, d_kb_s[1][256:272])
    tap_sums = tap_sums + jnp.concatenate([b_sums, jnp.zeros_like(b_sums)], axis=1)
    conv_rows = []
    for k in range(CONV):
        conv_rows.append(
            jnp.sum(tap_sums[4 * k : 4 * k + 4] * table_s, axis=0, keepdims=True)
        )
    lane8 = iota((8, 128), 1)
    row8 = iota((8, 128), 0)
    last = jnp.zeros((8, 128), F32)
    head_total = 8 * heads
    for h in range(heads):
        at = slot * heads + h
        last = jnp.where((row8 == 0) & (lane8 == at), rate_grads[h], last)
        last = jnp.where((row8 == 0) & (lane8 == head_total + at), bias_grads[h], last)
    conv = jnp.concatenate(conv_rows, axis=0)
    pay_ref[...] = jnp.concatenate([conv[:, :128], conv[:, 128:], last], axis=0)


def mixer(args, place, loss_scale, interpret=False):
    (tokens, rc_map, embedding, norm_gain, w_values, w_gates, w_states, w_steps, conv_values,
     conv_states, step_bias, log_rate, skip_gain, head_gain, cotangent) = args
    own, inner = cotangent.shape
    chunks = tokens.shape[0]

    def body(*refs):
        mixer_kernel(place, *refs, loss_scale=loss_scale)

    return pl.pallas_call(
        body,
        out_shape=(
            jax.ShapeDtypeStruct((own, inner), BF16),
            jax.ShapeDtypeStruct((16, 128), F32),
        ),
        in_specs=[SM] * 4 + [VM] * 11,
        out_specs=(VM, VM),
        scratch_shapes=[
            pltpu.VMEM((CONV, chunks, 128), F32),
            pltpu.VMEM((CONV, chunks, 128), F32),
            pltpu.VMEM((chunks, 128), F32),
            pltpu.VMEM((16 * chunks, 128), F32),
        ],
        compiler_params=pltpu.CompilerParams(vmem_limit_bytes=56 * 1024 * 1024),
        interpret=interpret,
        name="mixer",
    )(
        rc_map, step_bias, log_rate, skip_gain, tokens, embedding,
        norm_gain.reshape(1, -1), w_values, w_gates, w_states, w_steps, conv_values, conv_states,
        head_gain.reshape(1, -1), cotangent,
    )


def gather_kernel(tok_ref, out_ref, held, send_sem, recv_sem):
    count = held.shape[0]
    me = lax.axis_index("ctx")
    barrier = pltpu.get_barrier_semaphore()

    def greet(k, carry):
        peer = lax.rem(me + k, count)
        pl.semaphore_signal(barrier, inc=1, device_id={"ctx": peer}, device_id_type=MESH)
        return carry

    lax.fori_loop(1, count, greet, 0)
    pl.semaphore_wait(barrier, count - 1)

    def copy(k, source):
        peer = lax.rem(me + k, count)
        return pltpu.make_async_remote_copy(
            src_ref=tok_ref,
            dst_ref=held.at[source],
            send_sem=send_sem.at[k],
            recv_sem=recv_sem.at[source],
            device_id={"ctx": peer},
            device_id_type=MESH,
        )

    def send(k, carry):
        copy(k, me).start()
        return carry

    lax.fori_loop(1, count, send, 0)
    held[me] = tok_ref[...]

    def finish(k, carry):
        source = lax.rem(me + k, count)
        copy(k, source).wait_recv()
        copy(k, me).wait_send()
        return carry

    lax.fori_loop(1, count, finish, 0)
    out_ref[...] = held[...]


def gather(tokens, count):
    held = (count,) + tokens.shape
    return pl.pallas_call(
        gather_kernel,
        out_shape=jax.ShapeDtypeStruct(held, jnp.int32),
        in_specs=[VM],
        out_specs=VM,
        scratch_shapes=[
            pltpu.VMEM(held, jnp.int32),
            pltpu.SemaphoreType.DMA((count,)),
            pltpu.SemaphoreType.DMA((count,)),
        ],
        compiler_params=pltpu.CompilerParams(collective_id=0, has_side_effects=True),
        name="gather_tokens",
    )(tokens)


def reduce_kernel(x_size, z_size, pay_ref, rate_ref, bias_ref, conv_ref,
                  a_slots, b_slots, c_slots, sent, send_sem, recv_sem):
    ctx = lax.axis_index("ctx")
    tp = lax.axis_index("tp")
    x, z = ctx // z_size, lax.rem(ctx, z_size)
    stages = (
        (a_slots, tp, 8, lambda i: {"tp": i}),
        (b_slots, x, x_size, lambda i: {"ctx": i * z_size + z}),
        (c_slots, z, z_size, lambda i: {"ctx": x * z_size + i}),
    )
    barrier = pltpu.get_barrier_semaphore()
    peers = 0
    for slots, mine, size, device in stages:
        for k in range(1, size):
            pl.semaphore_signal(
                barrier, inc=1, device_id=device(lax.rem(mine + k, size)), device_id_type=MESH
            )
            peers += 1
    pl.semaphore_wait(barrier, peers)
    base = 0
    source = pay_ref
    for number, (slots, mine, size, device) in enumerate(stages):

        def copy(k, place):
            return pltpu.make_async_remote_copy(
                src_ref=source,
                dst_ref=slots.at[place],
                send_sem=send_sem.at[base + k],
                recv_sem=recv_sem.at[base + place],
                device_id=device(lax.rem(mine + k, size)),
                device_id_type=MESH,
            )

        for k in range(1, size):
            copy(k, mine).start()
        slots[mine] = source[...]
        for k in range(1, size):
            copy(k, lax.rem(mine + k, size)).wait_recv()
        summed = slots[0]
        for i in range(1, size):
            summed = summed + slots[i]
        for k in range(1, size):
            copy(k, mine).wait_send()
        if number < 2:
            sent[number] = summed
            source = sent.at[number]
        base += size
    heads = rate_ref.shape[1]
    rate_ref[...] = summed[8:9, 0:heads]
    bias_ref[...] = summed[8:9, heads : 2 * heads]
    conv_ref[...] = jnp.concatenate([summed[0:4], summed[4:8]], axis=1)


def reduce_all(pay, x_size, z_size, heads):
    def body(*refs):
        reduce_kernel(x_size, z_size, *refs)

    shape = pay.shape
    total = 8 + x_size + z_size
    return pl.pallas_call(
        body,
        out_shape=(
            jax.ShapeDtypeStruct((1, heads), F32),
            jax.ShapeDtypeStruct((1, heads), F32),
            jax.ShapeDtypeStruct((4, 256), F32),
        ),
        in_specs=[VM],
        out_specs=(VM, VM, VM),
        scratch_shapes=[
            pltpu.VMEM((8,) + shape, F32),
            pltpu.VMEM((x_size,) + shape, F32),
            pltpu.VMEM((z_size,) + shape, F32),
            pltpu.VMEM((2,) + shape, F32),
            pltpu.SemaphoreType.DMA((total,)),
            pltpu.SemaphoreType.DMA((total,)),
        ],
        compiler_params=pltpu.CompilerParams(collective_id=1, has_side_effects=True),
        name="reduce_grads",
    )(pay)


def solution(mesh):
    count = mesh.shape["ctx"]
    z_size = 8
    x_size = count // z_size

    def on_device(*args):
        tokens = args[0]
        own, inner = args[-1].shape
        everyone = gather(tokens.reshape(2, 128), count).reshape(2 * count, 128)
        loss_scale = 1.0 / math.sqrt(own * count * HEAD)

        def place():
            return lax.axis_index("ctx"), lax.axis_index("tp")

        encoded, pay = mixer((everyone,) + args[1:], place, loss_scale)
        heads = args[11].shape[0] * mesh.shape["tp"]
        rate, bias, conv = reduce_all(pay, x_size, z_size, heads)
        return encoded, rate.reshape(-1), bias.reshape(-1), conv

    tp = P("tp")
    cols = P(None, "tp")
    in_specs = (
        P("ctx"), P(), P(), P(), cols, cols, P(), cols, cols, P(), tp, tp, tp, tp, P("ctx", "tp"),
    )
    return jax.shard_map(
        on_device, mesh=mesh, in_specs=in_specs,
        out_specs=(P("ctx", "tp"), P(), P(), P()), check_vma=False,
    )
```

profile of v0, /device:TPU:1, one launch (start us, length us, event | category | flops | bytes accessed | tf_op | source)
XLA Modules:
  0.0 60.2 jit_solution(17763629836351471016)
XLA Ops:
  0.6 15.9 %gather_tokens.1 = s32[32,2,128]{2,1,0:T(2,128)} custom-call(s32[2,128]{1,0:T(2,128)} %bitcast.9), custom_call_target="tpu_custom_call" | custom-call | tf_op jit(solution)/shard_map/gather_tokens/pallas_call | solution.py:433
  16.6 1.8 %copy.19.refs_10_ = bf16[2048,4]{1,0:T(8,128)(2,1)} copy(bf16[2048,4]{0,1:T(4,128)(2,1)} %param.22) | data formatting | bytes 32768 | tf_op args[7]
  18.3 19.7 %mixer.1 = (bf16[256,512]{1,0:T(8,128)(2,1)}, f32[16,128]{1,0:T(8,128)}) custom-call(s32[4]{0:T(128)} %refs_0_.1, f32[4]{0:T(128)} %refs_1_.1, f32[4]{0:T(128)} %refs_2_.1, f32[4]{0:T(128)} %refs_3_.1, s32[64,128]{1,0:T(8,128)} %bitcast.6, bf16[4,2048]{1,0:T(4,128)(2,1)} %refs_5_.1, f32[1,2048]{1,0:T(1,128)} %bitcast.7, bf16[2048,512]{1,0:T(8,128)(2,1)} %refs_7_.1, ...), custom_call_target="tpu_custom_call" | custom-call | tf_op jit(solution)/shard_map/mixer/pallas_call | solution.py:366
  38.0 18.6 %reduce_grads.1 = (f32[1,32]{1,0:T(1,128)}, f32[1,32]{1,0:T(1,128)}, f32[4,256]{1,0:T(4,128)}) custom-call(f32[16,128]{1,0:T(8,128)} %get-tuple-element.10.refs_0_), custom_call_target="tpu_custom_call" | custom-call | tf_op jit(solution)/shard_map/reduce_grads/pallas_call | solution.py:507
  56.6 1.2 %copy.23 = f32[32]{0:T(128)} copy(f32[32]{0:T(128)} %bitcast.11) | data formatting | bytes 256
  57.8 1.1 %copy.24 = f32[32]{0:T(128)} copy(f32[32]{0:T(128)} %bitcast.10) | data formatting | bytes 256
  59.0 1.3 %copy.25 = f32[4,256]{1,0:T(4,128)} copy(f32[4,256]{1,0:T(4,128)} %get-tuple-element.21) | data formatting | bytes 8192
where the time goes:
time: 60.5 us; the launch traced here: 60.2 us
  Pallas kernels  54.2 us (90%)
  local copies, waits for them, and re-layouts  5.34 us (9%)
  between operations  0.65 us (1%)
    pallas_call x1, Pallas kernels, mixer(): pl.pallas_call(body, out_shape=(jax.ShapeDtypeStruct((own, inner), BF16),...  19.7 us
    pallas_call x1, Pallas kernels, reduce_all(): pl.pallas_call(body, out_shape=(jax.ShapeDtypeStruct((1, heads), F32), ja...  18.6 us
    pallas_call x1, Pallas kernels, gather(): pl.pallas_call(gather_kernel, out_shape=jax.ShapeDtypeStruct(held, jnp.in...  15.9 us
    unnamed x4, local copies, waits for them, and re-layouts  5.34 us

commit v1 on v0

--- a/solution.py
+++ b/solution.py
@@ -55,26 +55,142 @@
     return jnp.maximum(v, 0.0) + jnp.log1p(jnp.exp(-jnp.abs(v)))
 
 
-def mixer_kernel(
-    place, rc, bias, log_rate, skip, tok_ref, emb_ref, ng_ref, wv_ref, wg_ref, ws_ref, wst_ref,
-    cv_ref, cs_ref, hg_ref, cot_ref, enc_ref, pay_ref, fwd_ref, rev_ref, kmer_ref, rows_ref,
+class Links:
+    def __init__(self, refs, z_size):
+        (self.held, self.slots, self.sent, self.tok_send, self.tok_recv, self.sum_send,
+         self.sum_recv) = refs
+        self.z_size = z_size
+        self.count = self.held.shape[0]
+        self.ctx = lax.axis_index("ctx")
+        self.tp = lax.axis_index("tp")
+        self.tp_size = 8
+
+    def greet(self):
+        barrier = pltpu.get_barrier_semaphore()
+
+        def along_ctx(k, carry):
+            peer = lax.rem(self.ctx + k, self.count)
+            pl.semaphore_signal(barrier, inc=1, device_id={"ctx": peer}, device_id_type=MESH)
+            return carry
+
+        def along_tp(k, carry):
+            peer = lax.rem(self.tp + k, self.tp_size)
+            pl.semaphore_signal(barrier, inc=1, device_id={"tp": peer}, device_id_type=MESH)
+            return carry
+
+        lax.fori_loop(1, self.count, along_ctx, 0)
+        lax.fori_loop(1, self.tp_size, along_tp, 0)
+
+    def met(self):
+        pl.semaphore_wait(pltpu.get_barrier_semaphore(), self.count + self.tp_size - 2)
+
+    def token_copy(self, tok_ref, k, source):
+        return pltpu.make_async_remote_copy(
+            src_ref=tok_ref,
+            dst_ref=self.held.at[source],
+            send_sem=self.tok_send.at[k],
+            recv_sem=self.tok_recv.at[source],
+            device_id={"ctx": lax.rem(self.ctx + k, self.count)},
+            device_id_type=MESH,
+        )
+
+    def send_tokens(self, tok_ref):
+        def send(k, carry):
+            self.token_copy(tok_ref, k, self.ctx).start()
+            return carry
+
+        lax.fori_loop(1, self.count, send, 0)
+        self.held[self.ctx] = tok_ref[...]
+
+    def take_tokens(self, tok_ref):
+        def take(k, carry):
+            self.token_copy(tok_ref, k, lax.rem(self.ctx + k, self.count)).wait_recv()
+            return carry
+
+        lax.fori_loop(1, self.count, take, 0)
+
+    def drain_tokens(self, tok_ref):
+        def drain(k, carry):
+            self.token_copy(tok_ref, k, self.ctx).wait_send()
+            return carry
+
+        lax.fori_loop(1, self.count, drain, 0)
+
+    def reduce(self, value):
+        x, z = self.ctx // self.z_size, lax.rem(self.ctx, self.z_size)
+        x_size = self.count // self.z_size
+        stages = (
+            (self.tp, self.tp_size, lambda i: {"tp": i}),
+            (x, x_size, lambda i: {"ctx": i * self.z_size + z}),
+            (z, self.z_size, lambda i: {"ctx": x * self.z_size + i}),
+        )
+        base = 0
+        for number, (mine, size, device) in enumerate(stages):
+            self.sent[number] = value
+
+            def copy(k, place):
+                return pltpu.make_async_remote_copy(
+                    src_ref=self.sent.at[number],
+                    dst_ref=self.slots.at[base + place],
+                    send_sem=self.sum_send.at[base + k],
+                    recv_sem=self.sum_recv.at[base + place],
+                    device_id=device(lax.rem(mine + k, size)),
+                    device_id_type=MESH,
+                )
+
+            for k in range(1, size):
+                copy(k, mine).start()
+            self.slots[base + mine] = value
+            for k in range(1, size):
+                copy(k, lax.rem(mine + k, size)).wait_recv()
+            value = self.slots[base]
+            for i in range(1, size):
+                value = value + self.slots[base + i]
+            for k in range(1, size):
+                copy(k, mine).wait_send()
+            base += size
+        return value
+
+
+def layer_kernel(
+    place, links, rc, bias, log_rate, skip, tok_ref, emb_ref, ng_ref, cv_ref, cs_ref, hg_ref,
+    ws_hbm, wst_hbm, wv_hbm, wg_hbm, cot_hbm, enc_ref, pay_ref, held, fwd_ref, rev_ref, kmer_ref,
+    rows_ref, decay_ref, ws_ref, wst_ref, wv_ref, wg_ref, cot_ref, load_sem,
     *, loss_scale,
 ):
     me, slot = place()
-    chunks = tok_ref.shape[0]
-    blocks = chunks // 2
+    blocks = held.shape[0]
+    chunks = 2 * blocks
     inner = cv_ref.shape[1]
     heads = inner // HEAD
     own = cot_ref.shape[0]
+    loads = [
+        pltpu.make_async_copy(source, target, load_sem.at[n])
+        for n, (source, target) in enumerate((
+            (ws_hbm, ws_ref), (wst_hbm, wst_ref), (wv_hbm, wv_ref), (wg_hbm, wg_ref),
+            (cot_hbm, cot_ref),
+        ))
+    ]
+    for load in loads:
+        load.start()
+    if links is not None:
+        links.greet()
 
     e = emb_ref[...].astype(F32)
     scale = lax.rsqrt(jnp.mean(e * e, axis=1, keepdims=True) + EPS)
     normed = (e * scale * ng_ref[...]).astype(BF16)
     normed = jnp.concatenate([normed, jnp.zeros((12, e.shape[1]), BF16)], axis=0)
+    loads[0].wait()
+    table_s = dot(normed, ws_ref[...])[0:4]
+    loads[1].wait()
+    table_d = dot(normed, wst_ref[...], 1, 1)[0:4]
+    loads[2].wait()
     table_v = dot(normed, wv_ref[...])[0:4]
-    table_s = dot(normed, ws_ref[...])[0:4]
+    if links is not None:
+        links.met()
+        links.send_tokens(tok_ref)
+    loads[3].wait()
     table_z = dot(normed, wg_ref[...])[0:4]
-    table_d = dot(normed, wst_ref[...])[0:4]
     lane_h = iota((1, heads), 1)
     bias_row = jnp.zeros((1, heads), F32)
     rate_row = jnp.zeros((1, heads), F32)
@@ -102,7 +218,57 @@
     p_low = (p_rest - p_mid.astype(F32)).astype(BF16)
     per_tap3 = jnp.concatenate([p_hi, p_mid, p_low], axis=0)
 
-    tok = tok_ref[...].astype(F32)
+    column = iota((256, 48), 1) % 16
+    digit = lax.shift_right_logical(iota((256, 48), 0), 2 * (3 - column // 4)) & 3
+    kmer_hits = (digit == column % 4).astype(F32).astype(BF16)
+    kmer_full = dot(kmer_hits, per_tap3)
+
+    width = inner + 2 * HEAD
+    tri_in = (iota((own, own), 0) <= iota((own, own), 1)).astype(BF16)
+    tri_out = (iota((own, own), 0) >= iota((own, own), 1)).astype(BF16)
+    pad4 = jnp.zeros((12, own), BF16)
+    mine = tok_ref[...].astype(F32)
+    mine = jnp.concatenate([mine[0:1], mine[1:2]], axis=1)
+    mine_rc = jnp.zeros_like(mine)
+    for a in range(4):
+        mine_rc = jnp.where(mine == a, rc[a].astype(F32), mine_rc)
+    letters = iota((4, own), 0).astype(F32)
+    own_f = (jnp.broadcast_to(mine, (4, own)) == letters).astype(F32)
+    own_r = (jnp.broadcast_to(mine_rc, (4, own)) == letters).astype(F32)
+    n_f = dot(jnp.concatenate([own_f.astype(BF16), pad4], axis=0), tri_in)
+    n_r = dot(jnp.concatenate([own_r.astype(BF16), pad4], axis=0), tri_out)
+    cum_rows, sig_rows, step_rows, own_sig = [], [], [], []
+    for counted, hit in ((n_f, own_f), (n_r, own_r)):
+        for h in range(heads):
+            steps_sum = sum(counted[a : a + 1] * step_t[a : a + 1, h : h + 1] for a in range(4))
+            cum_rows.append(-(rate_row[:, h : h + 1] * steps_sum))
+            sig_rows.append(
+                sum(counted[a : a + 1] * sig_t[a : a + 1, h : h + 1] for a in range(4))
+            )
+            step_rows.append(sum(hit[a : a + 1] * step_t[a : a + 1, h : h + 1] for a in range(4)))
+            own_sig.append(sum(hit[a : a + 1] * sig_t[a : a + 1, h : h + 1] for a in range(4)))
+    stack = jnp.concatenate(
+        cum_rows + sig_rows + [jnp.zeros((128 - 4 * heads, own), F32)], axis=0
+    )
+    columns = jnp.transpose(stack)
+    for n in range(2 * heads):
+        if n < heads:
+            causal = iota((own, own), 0) >= iota((own, own), 1)
+        else:
+            causal = iota((own, own), 0) <= iota((own, own), 1)
+        decay_ref[n] = (
+            jnp.where(causal, jnp.exp(columns[:, n : n + 1] - cum_rows[n]), 0.0) * step_rows[n]
+        )
+    loads[4].wait()
+    gain = hg_ref[...]
+    cot_ref32 = cot_ref[...].astype(F32) * loss_scale
+
+    if links is not None:
+        links.take_tokens(tok_ref)
+    for r in range(blocks):
+        kmer_ref[2 * r : 2 * r + 2, :] = held[r].astype(F32)
+
+    tok = kmer_ref[...]
     comp = jnp.zeros_like(tok)
     for a in range(4):
         comp = jnp.where(tok == a, rc[a].astype(F32), comp)
@@ -194,12 +360,8 @@
     hits_t = jnp.concatenate([h.astype(F32) for h in hits_t], axis=0)
     hits3_t = jnp.concatenate([hits_t, hits_t, hits_t], axis=0).astype(BF16)
     local_sum = dot(hits3_t, per_tap3, 0, 0)
-    column = iota((256, 48), 1) % 16
-    digit = lax.shift_right_logical(iota((256, 48), 0), 2 * (3 - column // 4)) & 3
-    kmer_hits = (digit == column % 4).astype(F32).astype(BF16)
-    kmer_sum = dot(kmer_hits, per_tap3)
     ends_sum = jnp.concatenate([local_sum[512:520], local_sum[632:640]], axis=0)
-    kmer_sum = jnp.concatenate([kmer_sum, ends_sum], axis=0)
+    kmer_sum = jnp.concatenate([kmer_full, ends_sum], axis=0)
 
     def silu(v):
         return v / (1.0 + jnp.exp(-v))
@@ -208,38 +370,13 @@
         s = 1.0 / (1.0 + jnp.exp(-v))
         return s + v * s * (1.0 - s)
 
-    width = inner + 2 * HEAD
     kx = silu(kmer_sum[:, :inner])
     kb = silu(kmer_sum[:, inner : inner + HEAD])
     k_steps = kmer_sum[:, width + inner : width + inner + 128]
     kx_s = [split(kx[:, h * HEAD : (h + 1) * HEAD]) for h in range(heads)]
     kb_s = split(kb)
 
-    tri_in = (iota((own, own), 0) <= iota((own, own), 1)).astype(BF16)
-    tri_out = (iota((own, own), 0) >= iota((own, own), 1)).astype(BF16)
-    pad4 = jnp.zeros((12, own), BF16)
-    hits_f = hits_t[12:16, 0:own].astype(BF16)
-    hits_r = hits_t[12:16, own : 2 * own].astype(BF16)
-    n_f = dot(jnp.concatenate([hits_f, pad4], axis=0), tri_in)
-    n_r = dot(jnp.concatenate([hits_r, pad4], axis=0), tri_out)
-    cum_rows, sig_rows, step_rows, own_sig = [], [], [], []
-    for counted, hit in ((n_f, hits_t[12:16, 0:own]), (n_r, hits_t[12:16, own : 2 * own])):
-        for h in range(heads):
-            steps_sum = sum(counted[a : a + 1] * step_t[a : a + 1, h : h + 1] for a in range(4))
-            cum_rows.append(-(rate_row[:, h : h + 1] * steps_sum))
-            sig_rows.append(
-                sum(counted[a : a + 1] * sig_t[a : a + 1, h : h + 1] for a in range(4))
-            )
-            step_rows.append(sum(hit[a : a + 1] * step_t[a : a + 1, h : h + 1] for a in range(4)))
-            own_sig.append(sum(hit[a : a + 1] * sig_t[a : a + 1, h : h + 1] for a in range(4)))
-    stack = jnp.concatenate(
-        cum_rows + sig_rows + [jnp.zeros((128 - 4 * heads, own), F32)], axis=0
-    )
-    columns = jnp.transpose(stack)
-
-    cot = cot_ref[...].astype(F32) * loss_scale
-    gain = hg_ref[...]
-    encoded = jnp.zeros((own, inner), F32)
+    cot = cot_ref32
     d_kb = jnp.zeros(kb.shape, F32)
     rate_grads = [jnp.zeros((1, 1), F32)] * heads
     bias_grads = [jnp.zeros((1, 1), F32)] * heads
@@ -258,10 +395,6 @@
         c = states[:, HEAD:]
         c_s = split(c)
         scores = mm(c_s, b_s, 1, 1)
-        if strand == 0:
-            causal = iota((own, own), 0) >= iota((own, own), 1)
-        else:
-            causal = iota((own, own), 0) <= iota((own, own), 1)
         d_scores = jnp.zeros((own, own), F32)
         d_c = jnp.zeros((own, HEAD), F32)
         for h in range(heads):
@@ -278,7 +411,7 @@
             cum_c = columns[:, n : n + 1]
             sig_c = columns[:, 2 * heads + n : 2 * heads + n + 1]
             cum_r, sig_r, step_r = cum_rows[n], sig_rows[n], step_rows[n]
-            decays = jnp.where(causal, jnp.exp(cum_c - cum_r), 0.0) * step_r
+            decays = decay_ref[n]
             x_h = x[:, part]
             x_s = split(x_h)
             grow = jnp.exp(cum_c)
@@ -289,7 +422,6 @@
             inv = lax.rsqrt(jnp.mean(gated * gated, axis=1, keepdims=True) + EPS)
             normal = gated * inv
             out = normal * gain[:, part]
-            enc_part = encoded[:, part] + out
             if strand == 0:
                 rows_ref[h * own : (h + 1) * own, :] = out
             else:
@@ -351,198 +483,120 @@
         last = jnp.where((row8 == 0) & (lane8 == at), rate_grads[h], last)
         last = jnp.where((row8 == 0) & (lane8 == head_total + at), bias_grads[h], last)
     conv = jnp.concatenate(conv_rows, axis=0)
-    pay_ref[...] = jnp.concatenate([conv[:, :128], conv[:, 128:], last], axis=0)
-
-
-def mixer(args, place, loss_scale, interpret=False):
+    value = jnp.concatenate([conv[:, :128], conv[:, 128:], last], axis=0)
+    if links is not None:
+        links.drain_tokens(tok_ref)
+        value = links.reduce(value)
+    pay_ref[...] = value
+
+
+def layer(args, place, loss_scale, z_size, everyone=None):
     (tokens, rc_map, embedding, norm_gain, w_values, w_gates, w_states, w_steps, conv_values,
      conv_states, step_bias, log_rate, skip_gain, head_gain, cotangent) = args
     own, inner = cotangent.shape
-    chunks = tokens.shape[0]
+    blocks = everyone.shape[0] if everyone is not None else 4 * z_size
+    chunks = 2 * blocks
+    hbm = pl.BlockSpec(memory_space=pl.ANY)
+
+    scratch = [
+        pltpu.VMEM((CONV, chunks, 128), F32),
+        pltpu.VMEM((CONV, chunks, 128), F32),
+        pltpu.VMEM((chunks, 128), F32),
+        pltpu.VMEM((16 * chunks, 128), F32),
+        pltpu.VMEM((8, own, own), F32),
+        pltpu.VMEM(w_states.shape, BF16),
+        pltpu.VMEM(w_steps.shape[::-1], BF16),
+        pltpu.VMEM(w_values.shape, BF16),
+        pltpu.VMEM(w_gates.shape, BF16),
+        pltpu.VMEM(cotangent.shape, BF16),
+        pltpu.SemaphoreType.DMA((5,)),
+    ]
+    stages = 8 + blocks // z_size + z_size
+    remote = [
+        pltpu.VMEM((blocks, 2, 128), jnp.int32),
+        pltpu.VMEM((stages, 16, 128), F32),
+        pltpu.VMEM((3, 16, 128), F32),
+        pltpu.SemaphoreType.DMA((blocks,)),
+        pltpu.SemaphoreType.DMA((blocks,)),
+        pltpu.SemaphoreType.DMA((stages,)),
+        pltpu.SemaphoreType.DMA((stages,)),
+    ]
+    small = [
+        rc_map, step_bias, log_rate, skip_gain, tokens, embedding, norm_gain.reshape(1, -1),
+        conv_values, conv_states, head_gain.reshape(1, -1),
+    ]
+    large = [w_states, w_steps.T, w_values, w_gates, cotangent]
+    shapes = (
+        jax.ShapeDtypeStruct((own, inner), BF16),
+        jax.ShapeDtypeStruct((16, 128), F32),
+    )
+    if everyone is not None:
+
+        def body(*refs):
+            held = refs[10]
+            layer_kernel(
+                place, None, *refs[:10], *refs[11:18], held, *refs[18:], loss_scale=loss_scale
+            )
+
+        return pl.pallas_call(
+            body, out_shape=shapes, in_specs=[SM] * 4 + [VM] * 7 + [hbm] * 5, out_specs=(VM, VM),
+            scratch_shapes=scratch, interpret=True,
+        )(*small, everyone, *large)
 
     def body(*refs):
-        mixer_kernel(place, *refs, loss_scale=loss_scale)
+        links = Links(refs[17:24], z_size)
+        layer_kernel(place, links, *refs[:17], refs[17], *refs[24:], loss_scale=loss_scale)
 
     return pl.pallas_call(
         body,
+        out_shape=shapes,
+        in_specs=[SM] * 4 + [VM] * 6 + [hbm] * 5,
+        out_specs=(VM, VM),
+        scratch_shapes=remote + scratch,
+        compiler_params=pltpu.CompilerParams(
+            vmem_limit_bytes=60 * 1024 * 1024, collective_id=0, has_side_effects=True
+        ),
+        name="layer",
+    )(*small, *large)
+
+
+def emit_kernel(enc_ref, pay_ref, out_ref, rate_ref, bias_ref, conv_ref):
+    heads = rate_ref.shape[1]
+    out_ref[...] = enc_ref[...]
+    rate_ref[...] = pay_ref[8:9, 0:heads]
+    bias_ref[...] = pay_ref[8:9, heads : 2 * heads]
+    conv_ref[...] = jnp.concatenate([pay_ref[0:4, :], pay_ref[4:8, :]], axis=1)
+
+
+def emit(encoded, pay, heads):
+    return pl.pallas_call(
+        emit_kernel,
         out_shape=(
-            jax.ShapeDtypeStruct((own, inner), BF16),
-            jax.ShapeDtypeStruct((16, 128), F32),
-        ),
-        in_specs=[SM] * 4 + [VM] * 11,
-        out_specs=(VM, VM),
-        scratch_shapes=[
-            pltpu.VMEM((CONV, chunks, 128), F32),
-            pltpu.VMEM((CONV, chunks, 128), F32),
-            pltpu.VMEM((chunks, 128), F32),
-            pltpu.VMEM((16 * chunks, 128), F32),
-        ],
-        compiler_params=pltpu.CompilerParams(vmem_limit_bytes=56 * 1024 * 1024),
-        interpret=interpret,
-        name="mixer",
-    )(
-        rc_map, step_bias, log_rate, skip_gain, tokens, embedding,
-        norm_gain.reshape(1, -1), w_values, w_gates, w_states, w_steps, conv_values, conv_states,
-        head_gain.reshape(1, -1), cotangent,
-    )
-
-
-def gather_kernel(tok_ref, out_ref, held, send_sem, recv_sem):
-    count = held.shape[0]
-    me = lax.axis_index("ctx")
-    barrier = pltpu.get_barrier_semaphore()
-
-    def greet(k, carry):
-        peer = lax.rem(me + k, count)
-        pl.semaphore_signal(barrier, inc=1, device_id={"ctx": peer}, device_id_type=MESH)
-        return carry
-
-    lax.fori_loop(1, count, greet, 0)
-    pl.semaphore_wait(barrier, count - 1)
-
-    def copy(k, source):
-        peer = lax.rem(me + k, count)
-        return pltpu.make_async_remote_copy(
-            src_ref=tok_ref,
-            dst_ref=held.at[source],
-            send_sem=send_sem.at[k],
-            recv_sem=recv_sem.at[source],
-            device_id={"ctx": peer},
-            device_id_type=MESH,
-        )
-
-    def send(k, carry):
-        copy(k, me).start()
-        return carry
-
-    lax.fori_loop(1, count, send, 0)
-    held[me] = tok_ref[...]
-
-    def finish(k, carry):
-        source = lax.rem(me + k, count)
-        copy(k, source).wait_recv()
-        copy(k, me).wait_send()
-        return carry
-
-    lax.fori_loop(1, count, finish, 0)
-    out_ref[...] = held[...]
-
-
-def gather(tokens, count):
-    held = (count,) + tokens.shape
-    return pl.pallas_call(
-        gather_kernel,
-        out_shape=jax.ShapeDtypeStruct(held, jnp.int32),
-        in_specs=[VM],
-        out_specs=VM,
-        scratch_shapes=[
-            pltpu.VMEM(held, jnp.int32),
-            pltpu.SemaphoreType.DMA((count,)),
-            pltpu.SemaphoreType.DMA((count,)),
-        ],
-        compiler_params=pltpu.CompilerParams(collective_id=0, has_side_effects=True),
-        name="gather_tokens",
-    )(tokens)
-
-
-def reduce_kernel(x_size, z_size, pay_ref, rate_ref, bias_ref, conv_ref,
-                  a_slots, b_slots, c_slots, sent, send_sem, recv_sem):
-    ctx = lax.axis_index("ctx")
-    tp = lax.axis_index("tp")
-    x, z = ctx // z_size, lax.rem(ctx, z_size)
-    stages = (
-        (a_slots, tp, 8, lambda i: {"tp": i}),
-        (b_slots, x, x_size, lambda i: {"ctx": i * z_size + z}),
-        (c_slots, z, z_size, lambda i: {"ctx": x * z_size + i}),
-    )
-    barrier = pltpu.get_barrier_semaphore()
-    peers = 0
-    for slots, mine, size, device in stages:
-        for k in range(1, size):
-            pl.semaphore_signal(
-                barrier, inc=1, device_id=device(lax.rem(mine + k, size)), device_id_type=MESH
-            )
-            peers += 1
-    pl.semaphore_wait(barrier, peers)
-    base = 0
-    source = pay_ref
-    for number, (slots, mine, size, device) in enumerate(stages):
-
-        def copy(k, place):
-            return pltpu.make_async_remote_copy(
-                src_ref=source,
-                dst_ref=slots.at[place],
-                send_sem=send_sem.at[base + k],
-                recv_sem=recv_sem.at[base + place],
-                device_id=device(lax.rem(mine + k, size)),
-                device_id_type=MESH,
-            )
-
-        for k in range(1, size):
-            copy(k, mine).start()
-        slots[mine] = source[...]
-        for k in range(1, size):
-            copy(k, lax.rem(mine + k, size)).wait_recv()
-        summed = slots[0]
-        for i in range(1, size):
-            summed = summed + slots[i]
-        for k in range(1, size):
-            copy(k, mine).wait_send()
-        if number < 2:
-            sent[number] = summed
-            source = sent.at[number]
-        base += size
-    heads = rate_ref.shape[1]
-    rate_ref[...] = summed[8:9, 0:heads]
-    bias_ref[...] = summed[8:9, heads : 2 * heads]
-    conv_ref[...] = jnp.concatenate([summed[0:4], summed[4:8]], axis=1)
-
-
-def reduce_all(pay, x_size, z_size, heads):
-    def body(*refs):
-        reduce_kernel(x_size, z_size, *refs)
-
-    shape = pay.shape
-    total = 8 + x_size + z_size
-    return pl.pallas_call(
-        body,
-        out_shape=(
+            jax.ShapeDtypeStruct(encoded.shape, BF16),
             jax.ShapeDtypeStruct((1, heads), F32),
             jax.ShapeDtypeStruct((1, heads), F32),
             jax.ShapeDtypeStruct((4, 256), F32),
         ),
-        in_specs=[VM],
-        out_specs=(VM, VM, VM),
-        scratch_shapes=[
-            pltpu.VMEM((8,) + shape, F32),
-            pltpu.VMEM((x_size,) + shape, F32),
-            pltpu.VMEM((z_size,) + shape, F32),
-            pltpu.VMEM((2,) + shape, F32),
-            pltpu.SemaphoreType.DMA((total,)),
-            pltpu.SemaphoreType.DMA((total,)),
-        ],
-        compiler_params=pltpu.CompilerParams(collective_id=1, has_side_effects=True),
-        name="reduce_grads",
-    )(pay)
+        in_specs=[VM] * 2,
+        out_specs=(VM,) * 4,
+        name="emit",
+    )(encoded, pay)
 
 
 def solution(mesh):
     count = mesh.shape["ctx"]
-    z_size = 8
-    x_size = count // z_size
+    z_size = count // 4
 
     def on_device(*args):
-        tokens = args[0]
-        own, inner = args[-1].shape
-        everyone = gather(tokens.reshape(2, 128), count).reshape(2 * count, 128)
+        own = args[-1].shape[0]
         loss_scale = 1.0 / math.sqrt(own * count * HEAD)
 
         def place():
             return lax.axis_index("ctx"), lax.axis_index("tp")
 
-        encoded, pay = mixer((everyone,) + args[1:], place, loss_scale)
         heads = args[11].shape[0] * mesh.shape["tp"]
-        rate, bias, conv = reduce_all(pay, x_size, z_size, heads)
+        encoded, pay = layer((args[0].reshape(2, 128),) + args[1:], place, loss_scale, z_size)
+        encoded, rate, bias, conv = emit(encoded, pay, heads)
         return encoded, rate.reshape(-1), bias.reshape(-1), conv
 
     tp = P("tp")

time: 60.5 us -> 49.7 us (0.82)
  local copies, waits for them, and re-layouts: 5.34 us -> 0 us
  Pallas kernels: 54.2 us -> 48.9 us
    unnamed x4 -> x0, local copies, waits for them, and re-layouts: 5.34 us -> none
    pallas_call x3 -> x2, Pallas kernels: 54.2 us -> 48.9 us  [the longest x1 47.2 us: layer(): pl.pallas_call(body, out_shape=shapes, in_specs=[SM] * 4 + [VM] * 6 + [hb...]
where the time goes in v1:
time: 49.7 us; the launch traced here: 49.5 us
  Pallas kernels  48.9 us (98%)
  between operations  0.65 us (1%)
    pallas_call x1, Pallas kernels, layer(): pl.pallas_call(body, out_shape=shapes, in_specs=[SM] * 4 + [VM] * 6 + [hb...  47.2 us
    pallas_call x1, Pallas kernels, emit(): pl.pallas_call(emit_kernel, out_shape=(jax.ShapeDtypeStruct(encoded.shape...  1.68 us

profile of v1, /device:TPU:1, one launch (start us, length us, event | category | flops | bytes accessed | tf_op | source)
XLA Modules:
  0.0 49.5 jit_solution(9353638736132236446)
XLA Ops:
  0.6 47.2 %layer.1 = (bf16[256,512]{1,0:T(8,128)(2,1)}, f32[16,128]{1,0:T(8,128)}) custom-call(s32[4]{0:T(128)} %refs_0_.1, f32[4]{0:T(128)} %refs_1_.1, f32[4]{0:T(128)} %refs_2_.1, f32[4]{0:T(128)} %refs_3_.1, s32[2,128]{1,0:T(2,128)} %bitcast.9, bf16[4,2048]{1,0:T(4,128)(2,1)} %refs_5_.1, f32[1,2048]{1,0:T(1,128)} %bitcast.7, f32[4,512]{1,0:T(4,128)} %refs_7_.1, ...), custom_call_target="tpu_custom_call" | custom-call | tf_op jit(solution)/shard_map/layer/pallas_call | solution.py:550
  47.9 1.7 %emit.1 = (bf16[256,512]{1,0:T(8,128)(2,1)}, f32[1,32]{1,0:T(1,128)}, f32[1,32]{1,0:T(1,128)}, f32[4,256]{1,0:T(4,128)}) custom-call(bf16[256,512]{1,0:T(8,128)(2,1)} %get-tuple-element.10.enc_ref, f32[16,128]{1,0:T(8,128)} %get-tuple-element.11.pay_ref), custom_call_target="tpu_custom_call" | custom-call | tf_op jit(solution)/shard_map/emit/pallas_call | solution.py:572

commit v2 on v1

v2 whole, which is shorter than its diff:
```python
import math

import jax
import jax.numpy as jnp
from jax import lax
from jax.experimental import pallas as pl
from jax.experimental.pallas import tpu as pltpu
from jax.sharding import PartitionSpec as P

F32 = jnp.float32
BF16 = jnp.bfloat16
HEAD = 128
CONV = 4
EPS = 1e-05
MESH = pl.DeviceIdType.MESH
VM = pl.BlockSpec(memory_space=pltpu.VMEM)
SM = pl.BlockSpec(memory_space=pltpu.SMEM)


def split(v):
    hi = v.astype(BF16)
    return hi, (v - hi.astype(F32)).astype(BF16)


def dot(a, b, ca=1, cb=0):
    return lax.dot_general(a, b, (((ca,), (cb,)), ((), ())), preferred_element_type=F32)


def lhs3(v):
    hi, lo = v
    return jnp.concatenate([hi, lo, hi], axis=1)


def rhs3(v, axis=0):
    hi, lo = v
    return jnp.concatenate([hi, hi, lo], axis=axis)


def silu(v):
    return v / (1.0 + jnp.exp(-v))


def silu_slope(v):
    s = 1.0 / (1.0 + jnp.exp(-v))
    return s + v * s * (1.0 - s)


def fold(v):
    return v[:, :128] + v[:, 128:]


def iota(shape, dim):
    return lax.broadcasted_iota(jnp.int32, shape, dim)


def back_one(v, fill):
    rolled = pltpu.roll(v, 1, 1)
    wrapped = pltpu.roll(rolled, 1, 0)
    moved = jnp.where(iota(v.shape, 1) == 0, wrapped, rolled)
    first = (iota(v.shape, 0) == 0) & (iota(v.shape, 1) == 0)
    return jnp.where(first, fill, moved)


def ahead_one(v, fill):
    rows, lanes = v.shape
    rolled = pltpu.roll(v, lanes - 1, 1)
    wrapped = pltpu.roll(rolled, rows - 1, 0)
    moved = jnp.where(iota(v.shape, 1) == lanes - 1, wrapped, rolled)
    last = (iota(v.shape, 0) == rows - 1) & (iota(v.shape, 1) == lanes - 1)
    return jnp.where(last, fill, moved)


def softplus(v):
    return jnp.maximum(v, 0.0) + jnp.log1p(jnp.exp(-jnp.abs(v)))


class Links:
    def __init__(self, refs, z_size):
        (self.held, self.slots, self.sent, self.tok_send, self.tok_recv, self.sum_send,
         self.sum_recv) = refs
        self.z_size = z_size
        self.count = self.held.shape[0]
        self.ctx = lax.axis_index("ctx")
        self.tp = lax.axis_index("tp")
        self.tp_size = 8
        self.x_size = self.count // z_size
        self.x, self.z = self.ctx // z_size, lax.rem(self.ctx, z_size)

    def greet(self):
        barrier = pltpu.get_barrier_semaphore()

        def along_ctx(k, carry):
            peer = lax.rem(self.ctx + k, self.count)
            pl.semaphore_signal(barrier, inc=1, device_id={"ctx": peer}, device_id_type=MESH)
            return carry

        def along_plane(k, carry):
            peer = lax.rem(self.tp + 1 + k // self.x_size, self.tp_size)
            row = lax.rem(k, self.x_size)
            where = {"ctx": row * self.z_size + self.z, "tp": peer}
            pl.semaphore_signal(barrier, inc=1, device_id=where, device_id_type=MESH)
            return carry

        lax.fori_loop(1, self.count, along_ctx, 0)
        lax.fori_loop(0, (self.tp_size - 1) * self.x_size, along_plane, 0)

    def met(self):
        pl.semaphore_wait(pltpu.get_barrier_semaphore(), self.count - 1 + (self.tp_size - 1) * self.x_size)

    def token_copy(self, tok_ref, k, source):
        return pltpu.make_async_remote_copy(
            src_ref=tok_ref,
            dst_ref=self.held.at[source],
            send_sem=self.tok_send.at[k],
            recv_sem=self.tok_recv.at[source],
            device_id={"ctx": lax.rem(self.ctx + k, self.count)},
            device_id_type=MESH,
        )

    def send_tokens(self, tok_ref):
        def send(k, carry):
            self.token_copy(tok_ref, k, self.ctx).start()
            return carry

        lax.fori_loop(1, self.count, send, 0)
        self.held[self.ctx] = tok_ref[...]

    def take_one(self, tok_ref, k):
        self.token_copy(tok_ref, k, lax.rem(self.ctx + k, self.count)).wait_recv()

    def take_neighbours(self, tok_ref):
        self.take_one(tok_ref, 1)
        self.take_one(tok_ref, self.count - 1)

    def take_others(self, tok_ref):
        def take(k, carry):
            self.take_one(tok_ref, k)
            return carry

        lax.fori_loop(2, self.count - 1, take, 0)

    def drain_tokens(self, tok_ref):
        def drain(k, carry):
            self.token_copy(tok_ref, k, self.ctx).wait_send()
            return carry

        lax.fori_loop(1, self.count, drain, 0)

    def reduce(self, value):
        plane = self.x_size * self.tp_size
        stages = (
            (
                self.x * self.tp_size + self.tp,
                plane,
                lambda i: {
                    "ctx": (i // self.tp_size) * self.z_size + self.z,
                    "tp": lax.rem(i, self.tp_size),
                },
            ),
            (self.z, self.z_size, lambda i: {"ctx": self.x * self.z_size + i}),
        )
        base = 0
        for number, (mine, size, device) in enumerate(stages):
            self.sent[number] = value

            def copy(k, place):
                return pltpu.make_async_remote_copy(
                    src_ref=self.sent.at[number],
                    dst_ref=self.slots.at[base + place],
                    send_sem=self.sum_send.at[base + k],
                    recv_sem=self.sum_recv.at[base + place],
                    device_id=device(lax.rem(mine + k, size)),
                    device_id_type=MESH,
                )

            def start(k, carry):
                copy(k, mine).start()
                return carry

            def take(k, carry):
                copy(k, lax.rem(mine + k, size)).wait_recv()
                return carry

            def drain(k, carry):
                copy(k, mine).wait_send()
                return carry

            lax.fori_loop(1, size, start, 0)
            self.slots[base + mine] = value
            lax.fori_loop(1, size, take, 0)
            value = self.slots[base]
            for i in range(1, size):
                value = value + self.slots[base + i]
            lax.fori_loop(1, size, drain, 0)
            base += size
        return value


def layer_kernel(
    place, links, rc, bias, log_rate, skip, tok_ref, emb_ref, ng_ref, cv_ref, cs_ref, hg_ref,
    ws_hbm, wst_hbm, wv_hbm, wg_hbm, cot_hbm, enc_ref, pay_ref, held, fwd_ref, rev_ref, kmer_ref,
    rows_ref, decay_ref, ws_ref, wst_ref, wv_ref, wg_ref, cot_ref, load_sem,
    xh_ref, xl_ref, y_ref, gate_ref, grow_ref, dg_ref, score_ref, gh_ref, gl_ref,
    *, loss_scale,
):
    me, slot = place()
    blocks = held.shape[0]
    chunks = 2 * blocks
    inner = cv_ref.shape[1]
    heads = inner // HEAD
    own = cot_ref.shape[0]
    width = inner + 2 * HEAD
    loads = [
        pltpu.make_async_copy(source, target, load_sem.at[n])
        for n, (source, target) in enumerate((
            (ws_hbm, ws_ref), (wst_hbm, wst_ref), (wv_hbm, wv_ref), (wg_hbm, wg_ref),
            (cot_hbm, cot_ref),
        ))
    ]
    for load in loads:
        load.start()
    if links is not None:
        links.greet()

    e = emb_ref[...].astype(F32)
    scale = lax.rsqrt(jnp.mean(e * e, axis=1, keepdims=True) + EPS)
    normed = (e * scale * ng_ref[...]).astype(BF16)
    normed = jnp.concatenate([normed, jnp.zeros((12, e.shape[1]), BF16)], axis=0)
    loads[0].wait()
    table_s = dot(normed, ws_ref[...])[0:4]
    loads[1].wait()
    table_d = dot(normed, wst_ref[...], 1, 1)[0:4]
    loads[2].wait()
    table_v = dot(normed, wv_ref[...])[0:4]
    if links is not None:
        links.met()
        links.send_tokens(tok_ref)
    loads[3].wait()
    table_z = dot(normed, wg_ref[...])[0:4]
    lane_h = iota((1, heads), 1)
    bias_row = jnp.zeros((1, heads), F32)
    rate_row = jnp.zeros((1, heads), F32)
    for h in range(heads):
        bias_row = jnp.where(lane_h == h, bias[h], bias_row)
        rate_row = jnp.where(lane_h == h, log_rate[h], rate_row)
    rate_row = jnp.exp(rate_row)
    pre_step = table_d + bias_row
    step_t = softplus(pre_step)
    sig_t = 1.0 / (1.0 + jnp.exp(-pre_step))
    ratio_t = jnp.where(step_t > 0.0, sig_t / step_t, 1.0)
    gate_t = silu(table_z)
    table_vs = jnp.concatenate([table_v, table_s], axis=1)
    taps = jnp.concatenate([cv_ref[...], cs_ref[...]], axis=1)
    none2 = jnp.zeros((4, 2 * heads), F32)
    rest = jnp.zeros((4, 128 - 3 * heads), F32)
    tail = jnp.concatenate(
        [
            gate_t,
            step_t, step_t, -rate_row * step_t, rest,
            none2, sig_t, rest,
            none2, ratio_t, rest,
        ],
        axis=1,
    )
    parts = []
    for k in range(CONV):
        last = tail if k == CONV - 1 else jnp.zeros_like(tail)
        parts.append(jnp.concatenate([table_vs * taps[k : k + 1], last], axis=1))
    per_tap = jnp.concatenate(parts, axis=0)
    p_hi = per_tap.astype(BF16)
    p_rest = per_tap - p_hi.astype(F32)
    p_mid = p_rest.astype(BF16)
    p_low = (p_rest - p_mid.astype(F32)).astype(BF16)
    per_tap3 = jnp.concatenate([p_hi, p_mid, p_low], axis=0)
    place_cols = width + inner

    column = iota((256, 48), 1) % 16
    digit = lax.shift_right_logical(iota((256, 48), 0), 2 * (3 - column // 4)) & 3
    kmer_hits = (digit == column % 4).astype(F32).astype(BF16)
    kmer_sum = dot(kmer_hits, per_tap3[:, : inner + HEAD])
    kmer_tail = dot(kmer_hits, per_tap3[:, place_cols:])
    kx = silu(kmer_sum[:, :inner])
    kb = silu(kmer_sum[:, inner:])
    kb_slope = silu_slope(kmer_sum[:, inner:])

    tri_in = (iota((own, own), 0) <= iota((own, own), 1)).astype(BF16)
    tri_out = (iota((own, own), 0) >= iota((own, own), 1)).astype(BF16)
    pad4 = jnp.zeros((12, own), BF16)

    def complement(v):
        out = jnp.full(v.shape, -1.0, F32)
        for a in range(4):
            out = jnp.where(v == a, rc[a].astype(F32), out)
        return out

    pair = tok_ref[...].astype(F32)
    mine = jnp.concatenate([pair[0:1], pair[1:2]], axis=1)
    mine_rc = complement(mine)
    letters = iota((4, own), 0).astype(F32)
    own_f = (jnp.broadcast_to(mine, (4, own)) == letters).astype(F32)
    own_r = (jnp.broadcast_to(mine_rc, (4, own)) == letters).astype(F32)
    n_f = dot(jnp.concatenate([own_f.astype(BF16), pad4], axis=0), tri_in)
    n_r = dot(jnp.concatenate([own_r.astype(BF16), pad4], axis=0), tri_out)

    def blend(weights, table, h):
        return sum(weights[a : a + 1] * table[a : a + 1, h : h + 1] for a in range(4))

    cum_rows, sig_rows, step_rows, ratio_rows = [], [], [], []
    for counted, hit in ((n_f, own_f), (n_r, own_r)):
        for h in range(heads):
            cum_rows.append(-(rate_row[:, h : h + 1] * blend(counted, step_t, h)))
            sig_rows.append(blend(counted, sig_t, h))
            step_rows.append(blend(hit, step_t, h))
            ratio_rows.append(blend(hit, ratio_t, h))
    cum8 = jnp.concatenate(cum_rows, axis=0)
    both = split(jnp.concatenate([cum8] + sig_rows, axis=0))
    side = jnp.concatenate([both[0], both[1]], axis=0)
    side = jnp.concatenate([side, side], axis=1)
    columns = jnp.transpose(
        jnp.concatenate([cum8, jnp.zeros((128 - 2 * heads, own), F32)], axis=0)
    )
    for n in range(2 * heads):
        if n < heads:
            causal = iota((own, own), 0) >= iota((own, own), 1)
        else:
            causal = iota((own, own), 0) <= iota((own, own), 1)
        cum_c = jnp.broadcast_to(columns[:, n : n + 1], (own, 128))
        for half in range(own // 128):
            at = slice(half * 128, half * 128 + 128)
            decay_ref[n, :, at] = (
                jnp.where(causal[:, at], jnp.exp(cum_c - cum_rows[n][:, at]), 0.0)
                * step_rows[n][:, at]
            )
        part = slice((n % heads) * HEAD, (n % heads + 1) * HEAD)
        grow_ref[n // heads, :, part] = jnp.exp(cum_c)
    loads[4].wait()
    gain = hg_ref[...]
    dg_ref[...] = cot_ref[...].astype(F32) * (gain * loss_scale)

    if links is not None:
        links.take_neighbours(tok_ref)
    earlier = held[lax.rem(me + blocks - 1, blocks)].astype(F32)[1:2]
    later = held[lax.rem(me + 1, blocks)].astype(F32)[0:1]
    earlier = jnp.where(me > 0, earlier, -1.0)
    later = jnp.where(me < blocks - 1, later, -1.0)
    line = jnp.concatenate([earlier, mine, later], axis=1)
    line = jnp.broadcast_to(line, (8, line.shape[1]))
    line_rc = complement(line)
    letters8 = iota((8, own), 0).astype(F32)
    f_hits, r_hits = [], []
    for k in range(CONV):
        d = CONV - 1 - k
        f_line = pltpu.roll(line, d, 1) if d else line
        r_line = pltpu.roll(line_rc, line.shape[1] - d, 1) if d else line_rc
        f_hits.append((f_line[:, 128 : 128 + own] == letters8)[0:4].astype(F32))
        r_hits.append((r_line[:, 128 : 128 + own] == letters8)[0:4].astype(F32))
    hits_t = [jnp.concatenate(f_hits, axis=0), jnp.concatenate(r_hits, axis=0)]
    slopes, c_parts, ct_parts, b_parts = [], [], [], []
    for strand in range(2):
        hits = jnp.concatenate([hits_t[strand]] * 3, axis=0).astype(BF16)
        summed = dot(hits, per_tap3[:, :place_cols], 0, 0)
        gate_ref[strand] = summed[:, width:]
        states = silu(summed[:, inner:width])
        slopes.append(silu_slope(summed[:, inner:width]))
        b_s = split(states[:, :HEAD])
        c_s = split(states[:, HEAD:])
        b_parts.append(b_s)
        c_parts.append(c_s)
        ct_parts.append(split(jnp.transpose(states[:, HEAD:])))
        scores = dot(lhs3(c_s), rhs3(b_s, 1), 1, 1)
        score_ref[strand] = scores
        for h in range(heads):
            part = slice(h * HEAD, (h + 1) * HEAD)
            x_h = silu(summed[:, part])
            x_s = split(x_h)
            xh_ref[strand, :, part] = x_s[0]
            xl_ref[strand, :, part] = x_s[1]
            mixing = split(scores * decay_ref[strand * heads + h])
            y_ref[strand, :, part] = dot(lhs3(mixing), rhs3(x_s)) + skip[h] * x_h

    if links is not None:
        links.take_others(tok_ref)
    for r in range(blocks):
        kmer_ref[2 * r : 2 * r + 2, :] = held[r].astype(F32)
    tok = kmer_ref[...]
    comp = complement(tok)
    f_shift, r_shift = [tok], [comp]
    for _ in range(CONV - 1):
        f_shift.append(back_one(f_shift[-1], -1.0))
        r_shift.append(ahead_one(r_shift[-1], -1.0))

    row = iota(tok.shape, 0)
    position = row * 128 + iota(tok.shape, 1)
    before = row < 2 * me
    outside = before | (row >= 2 * me + 2)
    kmer_f = f_shift[0] + 4.0 * f_shift[1] + 16.0 * f_shift[2] + 64.0 * f_shift[3]
    kmer_r = r_shift[0] + 4.0 * r_shift[1] + 16.0 * r_shift[2] + 64.0 * r_shift[3]
    kmer = jnp.where(before, kmer_f, kmer_r)
    edge = (before & (position < CONV - 1)) | (position >= chunks * 128 - (CONV - 1))
    kmer_ref[...] = jnp.where(edge & outside, -1.0, kmer)
    mixed = jnp.where(outside, jnp.where(before, tok, comp), -1.0)
    tri = (iota((128, 128), 0) <= iota((128, 128), 1)).astype(BF16)
    ones = jnp.ones((128, 128), BF16)
    strict = (iota((chunks, chunks), 1) < iota((chunks, chunks), 0)).astype(BF16)
    counts = []
    for a in range(4):
        hit = (mixed == a).astype(F32)
        hit16 = hit.astype(BF16)
        within = dot(hit16, tri)
        offset = dot(strict, dot(hit16, ones).astype(BF16))
        total_f = jnp.sum(jnp.where(before, hit, 0.0), keepdims=True)
        inclusive = within + offset - total_f
        counts.append(jnp.where(before, -inclusive, inclusive - hit))
    for h in range(heads):
        steps_sum = sum(counts[a] * step_t[a : a + 1, h : h + 1] for a in range(4))
        sig_sum = sum(counts[a] * sig_t[a : a + 1, h : h + 1] for a in range(4))
        exponent = -(rate_row[:, h : h + 1] * steps_sum)
        decay = jnp.where(outside, jnp.exp(exponent), 0.0)
        for q, value in enumerate((decay, decay * exponent, decay * sig_sum)):
            base = (q * heads + h) * chunks
            rows_ref[base : base + chunks, :] = value
    for q in range(3 * heads, 16):
        rows_ref[q * chunks : (q + 1) * chunks, :] = jnp.zeros((chunks, 128), F32)

    kmer_id = iota((256, 128), 0).astype(F32)
    idle = jnp.zeros((64, 256), BF16)

    def load_rows(chunk):
        return rows_ref[pl.ds(chunk, 16, stride=chunks), :]

    def one_hot(chunk):
        return (jnp.broadcast_to(kmer_ref[pl.ds(chunk, 1), :], (256, 128)) == kmer_id).astype(F32)

    def add_block(i, acc):
        weights = jnp.concatenate([load_rows(2 * i), load_rows(2 * i + 1)], axis=1)
        w_f = split(jnp.where(i < me, weights, 0.0))
        w_r = split(jnp.where(i > me, weights, 0.0))
        stacked = jnp.concatenate([w_f[0], w_f[1], w_r[0], w_r[1], idle], axis=0)
        hits = jnp.concatenate([one_hot(2 * i), one_hot(2 * i + 1)], axis=1).astype(BF16)
        return acc + dot(hits, stacked, 1, 1)

    acc = lax.fori_loop(0, blocks, add_block, jnp.zeros((256, 128), F32), unroll=4)
    lane = iota((16, 128), 1)
    e_f = split(jnp.where(lane < CONV - 1, load_rows(0), 0.0))
    e_r = split(jnp.where(lane >= 128 - (CONV - 1), load_rows(chunks - 1), 0.0))
    edge_rows = jnp.concatenate(
        [e_f[0], e_f[1], e_r[0], e_r[1], jnp.zeros((64, 128), BF16)], axis=0
    )
    pick_row = iota((16, 128), 0)
    pick = (lane == jnp.where(pick_row < 8, pick_row, pick_row + 112)).astype(BF16)
    acc = jnp.concatenate([acc, dot(pick, edge_rows, 1, 1)], axis=0)

    end_hits = []
    for k in range(CONV):
        d = CONV - 1 - k
        ends = jnp.where(
            iota((1, 128), 1) < 64, f_shift[d][0:1, :], r_shift[d][chunks - 1 : chunks, :]
        )
        end_hits.append(
            (jnp.broadcast_to(ends, (4, 128)) == iota((4, 128), 0).astype(F32)).astype(F32)
        )
    end_hits = jnp.concatenate(end_hits, axis=0).astype(BF16)
    end_pick = dot(end_hits, pick, 1, 1)
    end3 = jnp.concatenate([end_pick] * 3, axis=0).astype(BF16)
    end_sum = dot(end3, per_tap3, 0, 0)
    kx = jnp.concatenate([kx, silu(end_sum[:, :inner])], axis=0)
    kb = jnp.concatenate([kb, silu(end_sum[:, inner : inner + HEAD])], axis=0)
    kb_slope = jnp.concatenate([kb_slope, silu_slope(end_sum[:, inner : inner + HEAD])], axis=0)
    k_tail = jnp.concatenate([kmer_tail, end_sum[:, place_cols:]], axis=0)
    table_rows = kx.shape[0]

    joined = acc + pltpu.roll(acc, 128 - 16, 1)
    lanes = iota((1, 128), 1)
    lane_rate = jnp.zeros((1, 128), F32)
    for h in range(heads):
        lane_rate = jnp.where(lanes == 2 * heads + h, -rate_row[:, h : h + 1], lane_rate)
    lane_one = jnp.where((lanes >= heads) & (lanes < 2 * heads), 1.0, lane_rate)
    weights, ratios, kxw_parts = [], [], []
    for strand in range(2):
        source = joined if strand == 0 else pltpu.roll(joined, 128 - 32, 1)
        w = k_tail[:, 0:128] * source
        e4, e8 = pltpu.roll(source, heads, 1), pltpu.roll(source, 2 * heads, 1)
        decay = jnp.where((lanes >= heads) & (lanes < 2 * heads), e4, e8)
        kept = (decay > 0.0) & (lanes >= heads) & (lanes < 3 * heads)
        ratio = jnp.where(
            kept, lane_one * source / jnp.where(kept, decay, 1.0) + k_tail[:, 256:384], 0.0
        )
        ratio = jnp.concatenate(
            [ratio, jnp.zeros((384 - table_rows, 128), F32)], axis=0
        )
        ratio = split(jnp.transpose(ratio)[0:16, :table_rows])
        ratios.append(jnp.concatenate([ratio[0], ratio[1]], axis=0))
        kxw_parts.append(
            split(
                jnp.concatenate(
                    [
                        kx[:, h * HEAD : (h + 1) * HEAD]
                        * jnp.broadcast_to(w[:, h : h + 1], (table_rows, HEAD))
                        for h in range(heads)
                    ],
                    axis=1,
                )
            )
        )
    kb_t = jnp.concatenate([kb, jnp.zeros((384 - table_rows, HEAD), F32)], axis=0)
    kb_t = split(jnp.transpose(kb_t)[:, :table_rows])

    d_kb = jnp.zeros(kb.shape, F32)
    rate_grads = [jnp.zeros((1, 128), F32)] * heads
    bias_grads = [jnp.zeros((1, 128), F32)] * heads
    tap_sums = jnp.zeros((16, 2 * HEAD), F32)
    for strand in range(2):
        kxw = kxw_parts[strand]
        c_s, ct_s, b_s = c_parts[strand], ct_parts[strand], b_parts[strand]
        start = (
            dot(kb_t[0], kxw[0]) + (dot(kb_t[0], kxw[1]) + dot(kb_t[1], kxw[0]))
        )
        start_s = split(start)
        carried = dot(lhs3(c_s), rhs3(start_s))
        scores = score_ref[strand]
        d_scores = jnp.zeros((own, own), F32)
        for h in range(heads):
            n = strand * heads + h
            part = slice(h * HEAD, (h + 1) * HEAD)
            grow = grow_ref[strand, :, part]
            from_start = grow * carried[:, part]
            gate = gate_ref[strand, :, part]
            gated = (y_ref[strand, :, part] + from_start) * gate
            inv = lax.rsqrt(jnp.mean(gated * gated, axis=1, keepdims=True) + EPS)
            normal = gated * inv
            out = normal * gain[:, part]
            if strand == 0:
                y_ref[0, :, part] = out
            else:
                enc_ref[:, part] = (y_ref[0, :, part] + out).astype(BF16)
            d_normal = dg_ref[:, part]
            d_y = d_normal - normal * jnp.mean(normal * d_normal, axis=1, keepdims=True)
            d_y = (d_y * inv) * gate
            x_s = (xh_ref[strand, :, part], xl_ref[strand, :, part])
            mixed_grad = dot(lhs3(split(d_y)), rhs3(x_s, 1), 1, 1) * decay_ref[n]
            d_scores = d_scores + mixed_grad
            weighted = mixed_grad * scores
            wsum = split(fold(weighted) + d_y * from_start)
            moved = dot(side, jnp.concatenate([wsum[0], wsum[1]], axis=0))
            col_sum = jnp.sum(weighted, axis=0, keepdims=True)
            grown = split(d_y * grow)
            gh_ref[:, part] = grown[0]
            gl_ref[:, part] = grown[1]
            rate = rate_row[:, h : h + 1]
            rows = 2 * heads
            rate_grads[h] = (
                rate_grads[h]
                + (moved[n : n + 1] + moved[2 * rows + n : 2 * rows + n + 1])
                - fold(col_sum * cum_rows[n])
            )
            bias_grads[h] = (
                bias_grads[h]
                + fold(col_sum * (rate * sig_rows[n] + ratio_rows[n]))
                - rate * (moved[rows + n : rows + n + 1] + moved[3 * rows + n : 3 * rows + n + 1])
            )
        grown = (gh_ref[...], gl_ref[...])
        d_start = split(dot(lhs3(ct_s), rhs3(grown)))
        for h in range(heads):
            part = slice(h * HEAD, (h + 1) * HEAD)
            d_start_h = (d_start[0][:, part], d_start[1][:, part])
            pulled = dot(
                lhs3((kxw[0][:, part], kxw[1][:, part])), rhs3(d_start_h, 1), 1, 1
            )
            d_kb = d_kb + pulled
            t = split(pulled * kb)
            slope = dot(ratios[strand], t[0]) + dot(ratios[strand], t[1])
            slope = slope[0:16] + slope[16:32]
            rate_grads[h] = rate_grads[h] + slope[heads + h : heads + h + 1]
            bias_grads[h] = bias_grads[h] + slope[2 * heads + h : 2 * heads + h + 1]
        d_scores_s = split(d_scores)
        d_c = dot(lhs3(d_scores_s), rhs3(b_s)) + dot(lhs3(grown), rhs3(start_s, 1), 1, 1)
        d_b = dot(lhs3(split(jnp.transpose(d_scores))), rhs3(c_s))
        d_sum = split(jnp.concatenate([d_b, d_c], axis=1) * slopes[strand])
        hits = hits_t[strand].astype(BF16)
        tap_sums = tap_sums + dot(
            jnp.concatenate([hits, hits], axis=1), jnp.concatenate([d_sum[0], d_sum[1]], axis=0)
        )
    d_kb = split(d_kb * kb_slope)
    b_sums = dot(kmer_hits[:, 0:16], d_kb[0][0:256], 0, 0)
    b_sums = b_sums + dot(kmer_hits[:, 0:16], d_kb[1][0:256], 0, 0)
    end_pick = end_pick.astype(BF16)
    b_sums = b_sums + dot(end_pick, d_kb[0][256:]) + dot(end_pick, d_kb[1][256:])
    tap_sums = tap_sums + jnp.concatenate([b_sums, jnp.zeros_like(b_sums)], axis=1)
    conv_rows = []
    for k in range(CONV):
        conv_rows.append(
            jnp.sum(tap_sums[4 * k : 4 * k + 4] * table_s, axis=0, keepdims=True)
        )
    sums = jnp.sum(jnp.concatenate(rate_grads + bias_grads, axis=0), axis=1, keepdims=True)
    lane8 = iota((8, 128), 1)
    row8 = iota((8, 128), 0)
    last = jnp.zeros((8, 128), F32)
    head_total = 8 * heads
    for h in range(heads):
        at = slot * heads + h
        last = jnp.where((row8 == 0) & (lane8 == at), sums[h : h + 1], last)
        last = jnp.where(
            (row8 == 0) & (lane8 == head_total + at), sums[heads + h : heads + h + 1], last
        )
    conv = jnp.concatenate(conv_rows, axis=0)
    value = jnp.concatenate([conv[:, :128], conv[:, 128:], last], axis=0)
    if links is not None:
        links.drain_tokens(tok_ref)
        value = links.reduce(value)
    pay_ref[...] = value


def layer(args, place, loss_scale, z_size, everyone=None, interpret=False):
    (tokens, rc_map, embedding, norm_gain, w_values, w_gates, w_states, w_steps, conv_values,
     conv_states, step_bias, log_rate, skip_gain, head_gain, cotangent) = args
    own, inner = cotangent.shape
    blocks = everyone.shape[0] if everyone is not None else 4 * z_size
    chunks = 2 * blocks
    hbm = pl.BlockSpec(memory_space=pl.ANY)

    scratch = [
        pltpu.VMEM((CONV, chunks, 128), F32),
        pltpu.VMEM((CONV, chunks, 128), F32),
        pltpu.VMEM((chunks, 128), F32),
        pltpu.VMEM((16 * chunks, 128), F32),
        pltpu.VMEM((8, own, own), F32),
        pltpu.VMEM(w_states.shape, BF16),
        pltpu.VMEM(w_steps.shape[::-1], BF16),
        pltpu.VMEM(w_values.shape, BF16),
        pltpu.VMEM(w_gates.shape, BF16),
        pltpu.VMEM(cotangent.shape, BF16),
        pltpu.SemaphoreType.DMA((5,)),
        pltpu.VMEM((2, own, inner), BF16),
        pltpu.VMEM((2, own, inner), BF16),
        pltpu.VMEM((2, own, inner), F32),
        pltpu.VMEM((2, own, inner), F32),
        pltpu.VMEM((2, own, inner), F32),
        pltpu.VMEM((own, inner), F32),
        pltpu.VMEM((2, own, own), F32),
        pltpu.VMEM((own, inner), BF16),
        pltpu.VMEM((own, inner), BF16),
    ]
    stages = 8 * (blocks // z_size) + z_size
    remote = [
        pltpu.VMEM((blocks, 2, 128), jnp.int32),
        pltpu.VMEM((stages, 16, 128), F32),
        pltpu.VMEM((3, 16, 128), F32),
        pltpu.SemaphoreType.DMA((blocks,)),
        pltpu.SemaphoreType.DMA((blocks,)),
        pltpu.SemaphoreType.DMA((stages,)),
        pltpu.SemaphoreType.DMA((stages,)),
    ]
    small = [
        rc_map, step_bias, log_rate, skip_gain, tokens, embedding, norm_gain.reshape(1, -1),
        conv_values, conv_states, head_gain.reshape(1, -1),
    ]
    large = [w_states, w_steps.T, w_values, w_gates, cotangent]
    shapes = (
        jax.ShapeDtypeStruct((own, inner), BF16),
        jax.ShapeDtypeStruct((16, 128), F32),
    )
    if everyone is not None:

        def body(*refs):
            held = refs[10]
            layer_kernel(
                place, None, *refs[:10], *refs[11:18], held, *refs[18:], loss_scale=loss_scale
            )

        return pl.pallas_call(
            body, out_shape=shapes, in_specs=[SM] * 4 + [VM] * 7 + [hbm] * 5, out_specs=(VM, VM),
            scratch_shapes=scratch, interpret=interpret,
        )(*small, everyone, *large)

    def body(*refs):
        links = Links(refs[17:24], z_size)
        layer_kernel(place, links, *refs[:17], refs[17], *refs[24:], loss_scale=loss_scale)

    return pl.pallas_call(
        body,
        out_shape=shapes,
        in_specs=[SM] * 4 + [VM] * 6 + [hbm] * 5,
        out_specs=(VM, VM),
        scratch_shapes=remote + scratch,
        compiler_params=pltpu.CompilerParams(
            vmem_limit_bytes=60 * 1024 * 1024, collective_id=0, has_side_effects=True
        ),
        name="layer",
    )(*small, *large)


def emit_kernel(enc_ref, pay_ref, out_ref, rate_ref, bias_ref, conv_ref):
    heads = rate_ref.shape[1]
    out_ref[...] = enc_ref[...]
    rate_ref[...] = pay_ref[8:9, 0:heads]
    bias_ref[...] = pay_ref[8:9, heads : 2 * heads]
    conv_ref[...] = jnp.concatenate([pay_ref[0:4, :], pay_ref[4:8, :]], axis=1)


def emit(encoded, pay, heads):
    return pl.pallas_call(
        emit_kernel,
        out_shape=(
            jax.ShapeDtypeStruct(encoded.shape, BF16),
            jax.ShapeDtypeStruct((1, heads), F32),
            jax.ShapeDtypeStruct((1, heads), F32),
            jax.ShapeDtypeStruct((4, 256), F32),
        ),
        in_specs=[VM] * 2,
        out_specs=(VM,) * 4,
        name="emit",
    )(encoded, pay)


def solution(mesh):
    count = mesh.shape["ctx"]
    z_size = count // 4

    def on_device(*args):
        own = args[-1].shape[0]
        loss_scale = 1.0 / math.sqrt(own * count * HEAD)

        def place():
            return lax.axis_index("ctx"), lax.axis_index("tp")

        heads = args[11].shape[0] * mesh.shape["tp"]
        encoded, pay = layer((args[0].reshape(2, 128),) + args[1:], place, loss_scale, z_size)
        encoded, rate, bias, conv = emit(encoded, pay, heads)
        return encoded, rate.reshape(-1), bias.reshape(-1), conv

    tp = P("tp")
    cols = P(None, "tp")
    in_specs = (
        P("ctx"), P(), P(), P(), cols, cols, P(), cols, cols, P(), tp, tp, tp, tp, P("ctx", "tp"),
    )
    return jax.shard_map(
        on_device, mesh=mesh, in_specs=in_specs,
        out_specs=(P("ctx", "tp"), P(), P(), P()), check_vma=False,
    )
```

time: 49.7 us -> 46 us (0.926)
  Pallas kernels: 48.9 us -> 45.2 us
    pallas_call x1, Pallas kernels: 47.2 us -> 43.5 us  [layer(): pl.pallas_call(body, out_shape=shapes, in_specs=[SM] * 4 + [VM] * 6 + [hb...]
where the time goes in v2:
time: 46 us; the launch traced here: 45.9 us
  Pallas kernels  45.2 us (98%)
  between operations  0.65 us (1%)
    pallas_call x1, Pallas kernels, layer(): pl.pallas_call(body, out_shape=shapes, in_specs=[SM] * 4 + [VM] * 6 + [hb...  43.5 us
    pallas_call x1, Pallas kernels, emit(): pl.pallas_call(emit_kernel, out_shape=(jax.ShapeDtypeStruct(encoded.shape...  1.68 us

profile of v2, /device:TPU:1, one launch (start us, length us, event | category | flops | bytes accessed | tf_op | source)
XLA Modules:
  0.0 45.9 jit_solution(6516782241924431140)
XLA Ops:
  0.6 43.5 %layer.1 = (bf16[256,512]{1,0:T(8,128)(2,1)}, f32[16,128]{1,0:T(8,128)}) custom-call(s32[4]{0:T(128)} %refs_0_.1, f32[4]{0:T(128)} %refs_1_.1, f32[4]{0:T(128)} %refs_2_.1, f32[4]{0:T(128)} %refs_3_.1, s32[2,128]{1,0:T(2,128)} %bitcast.9, bf16[4,2048]{1,0:T(4,128)(2,1)} %refs_5_.1, f32[1,2048]{1,0:T(1,128)} %bitcast.7, f32[4,512]{1,0:T(4,128)} %refs_7_.1, ...), custom_call_target="tpu_custom_call" | custom-call | tf_op jit(solution)/shard_map/layer/pallas_call | solution.py:679
  44.2 1.7 %emit.1 = (bf16[256,512]{1,0:T(8,128)(2,1)}, f32[1,32]{1,0:T(1,128)}, f32[1,32]{1,0:T(1,128)}, f32[4,256]{1,0:T(4,128)}) custom-call(bf16[256,512]{1,0:T(8,128)(2,1)} %get-tuple-element.10.enc_ref, f32[16,128]{1,0:T(8,128)} %get-tuple-element.11.pay_ref), custom_call_target="tpu_custom_call" | custom-call | tf_op jit(solution)/shard_map/emit/pallas_call | solution.py:701

commit v3 on v2

v3 whole, which is shorter than its diff:
```python
import math

import jax
import jax.numpy as jnp
from jax import lax
from jax.experimental import pallas as pl
from jax.experimental.pallas import tpu as pltpu
from jax.sharding import PartitionSpec as P

F32 = jnp.float32
BF16 = jnp.bfloat16
HEAD = 128
CONV = 4
EPS = 1e-05
MESH = pl.DeviceIdType.MESH
VM = pl.BlockSpec(memory_space=pltpu.VMEM)


def split(v):
    hi = v.astype(BF16)
    return hi, (v - hi.astype(F32)).astype(BF16)


def dot(a, b, ca=1, cb=0):
    return lax.dot_general(a, b, (((ca,), (cb,)), ((), ())), preferred_element_type=F32)


def lhs3(v):
    hi, lo = v
    return jnp.concatenate([hi, lo, hi], axis=1)


def rhs3(v, axis=0):
    hi, lo = v
    return jnp.concatenate([hi, hi, lo], axis=axis)


def silu(v):
    return v / (1.0 + jnp.exp(-v))


def silu_slope(v):
    s = 1.0 / (1.0 + jnp.exp(-v))
    return s + v * s * (1.0 - s)


def fold(v):
    return v[:, :128] + v[:, 128:]


def iota(shape, dim):
    return lax.broadcasted_iota(jnp.int32, shape, dim)


def back_one(v, fill):
    rolled = pltpu.roll(v, 1, 1)
    wrapped = pltpu.roll(rolled, 1, 0)
    moved = jnp.where(iota(v.shape, 1) == 0, wrapped, rolled)
    first = (iota(v.shape, 0) == 0) & (iota(v.shape, 1) == 0)
    return jnp.where(first, fill, moved)


def ahead_one(v, fill):
    rows, lanes = v.shape
    rolled = pltpu.roll(v, lanes - 1, 1)
    wrapped = pltpu.roll(rolled, rows - 1, 0)
    moved = jnp.where(iota(v.shape, 1) == lanes - 1, wrapped, rolled)
    last = (iota(v.shape, 0) == rows - 1) & (iota(v.shape, 1) == lanes - 1)
    return jnp.where(last, fill, moved)


def softplus(v):
    return jnp.maximum(v, 0.0) + jnp.log1p(jnp.exp(-jnp.abs(v)))


SIZES = {"x": 4, "z": 8, "y": 4, "c": 2}


def offsets(axes):
    steps = [()]
    for axis in axes:
        steps = [step + (d,) for step in steps for d in range(SIZES[axis])]

    def hops(step):
        return sum(min(d, SIZES[axis] - d) for axis, d in zip(axes, step) if axis != "c")

    return sorted(steps[1:], key=lambda step: -hops(step))


class Links:
    def __init__(self, refs):
        (self.held, self.slots, self.sent, self.tok_send, self.tok_recv, self.sum_send,
         self.sum_recv) = refs
        ctx, tp = lax.axis_index("ctx"), lax.axis_index("tp")
        self.ctx = ctx
        self.here = {
            "x": ctx // SIZES["z"], "z": lax.rem(ctx, SIZES["z"]),
            "y": tp // SIZES["c"], "c": lax.rem(tp, SIZES["c"]),
        }
        self.drains = []

    def moved(self, axes, step):
        there = dict(self.here)
        for axis, d in zip(axes, step):
            if d:
                there[axis] = lax.rem(there[axis] + d, SIZES[axis])
        return there

    def device(self, there):
        return {
            "ctx": there["x"] * SIZES["z"] + there["z"], "tp": there["y"] * SIZES["c"] + there["c"]
        }

    def greet(self):
        barrier = pltpu.get_barrier_semaphore()
        self.greeted = 0
        plane = [step for step in offsets("xy") if step[1]]
        for axes, steps in (("xz", offsets("xz")), ("xy", plane), ("c", offsets("c"))):
            for step in steps:
                device = self.device(self.moved(axes, step))
                pl.semaphore_signal(barrier, inc=1, device_id=device, device_id_type=MESH)
                self.greeted += 1

    def met(self):
        pl.semaphore_wait(pltpu.get_barrier_semaphore(), self.greeted)

    def send_tokens(self, tok_ref):
        for k, step in enumerate(offsets("xz")):
            copy = pltpu.make_async_remote_copy(
                src_ref=tok_ref,
                dst_ref=self.held.at[self.ctx],
                send_sem=self.tok_send.at[k],
                recv_sem=self.tok_recv.at[self.ctx],
                device_id=self.device(self.moved("xz", step)),
                device_id_type=MESH,
            )
            copy.start()
            self.drains.append(copy)
        self.held[self.ctx] = tok_ref[...]

    def take_one(self, tok_ref, source):
        pltpu.make_async_remote_copy(
            src_ref=tok_ref,
            dst_ref=self.held.at[source],
            send_sem=self.tok_send.at[0],
            recv_sem=self.tok_recv.at[source],
            device_id={"ctx": source},
            device_id_type=MESH,
        ).wait_recv()

    def take_tokens(self, tok_ref, steps):
        count = self.held.shape[0]
        for k in steps:
            self.take_one(tok_ref, lax.rem(self.ctx + k, count))

    def reduce(self, value):
        base = 0
        for number, axes in enumerate(("c", "xy", "z")):
            self.sent[number] = value
            steps = offsets(axes)

            def slot(there):
                place = 0
                for axis in axes:
                    place = place * SIZES[axis] + there[axis]
                return base + place

            def copy(k, there, place):
                return pltpu.make_async_remote_copy(
                    src_ref=self.sent.at[number],
                    dst_ref=self.slots.at[place],
                    send_sem=self.sum_send.at[base + k],
                    recv_sem=self.sum_recv.at[place],
                    device_id=self.device(there),
                    device_id_type=MESH,
                )

            for k, step in enumerate(steps):
                sending = copy(k, self.moved(axes, step), slot(self.here))
                sending.start()
                self.drains.append(sending)
            self.slots[slot(self.here)] = value
            for step in reversed(steps):
                there = self.moved(axes, step)
                copy(0, there, slot(there)).wait_recv()
            value = self.slots[base]
            for i in range(1, len(steps) + 1):
                value = value + self.slots[base + i]
            base += len(steps) + 1
        return value

    def drain(self):
        for copy in self.drains:
            copy.wait_send()


def layer_kernel(
    place, links, sources, enc_hbm, pay_ref, held, stores, kmer_ref, last_ref, rows_ref, decay_ref, load_sem,
    xh_ref, xl_ref, y_ref, gate_ref, grow_ref, dg_ref, score_ref, gh_ref, gl_ref, car_ref, enc_ref,
    *, loss_scale,
):
    if links is not None:
        links.greet()
    loads = [
        pltpu.make_async_copy(source, store, load_sem.at[n])
        for n, (source, store) in enumerate(zip(sources, stores))
    ]
    for load in loads:
        load.start()
    (tok_ref, rc, bias, log_rate, skip, emb_ref, ng_ref, cv_ref, cs_ref, hg_ref, ws_ref, wst_ref,
     wv_ref, wg_ref, cot_ref) = stores
    me, slot = place()
    blocks = held.shape[0]
    chunks = 2 * blocks
    inner = cv_ref.shape[1]
    heads = inner // HEAD
    own = cot_ref.shape[0]
    width = inner + 2 * HEAD
    for load in loads[:10]:
        load.wait()
    e = emb_ref[...].astype(F32)
    scale = lax.rsqrt(jnp.mean(e * e, axis=1, keepdims=True) + EPS)
    normed = (e * scale * ng_ref[...]).astype(BF16)
    normed = jnp.concatenate([normed, jnp.zeros((12, e.shape[1]), BF16)], axis=0)
    loads[10].wait()
    table_s = dot(normed, ws_ref[...])[0:4]
    loads[11].wait()
    table_d = dot(normed, wst_ref[...], 1, 1)[0:4]
    loads[12].wait()
    table_v = dot(normed, wv_ref[...])[0:4]
    if links is not None:
        links.met()
        links.send_tokens(tok_ref)
    loads[13].wait()
    table_z = dot(normed, wg_ref[...])[0:4]
    lane_h = iota((1, heads), 1)
    bias_row = jnp.zeros((1, heads), F32)
    rate_row = jnp.zeros((1, heads), F32)
    for h in range(heads):
        bias_row = jnp.where(lane_h == h, bias[h], bias_row)
        rate_row = jnp.where(lane_h == h, log_rate[h], rate_row)
    rate_row = jnp.exp(rate_row)
    pre_step = table_d + bias_row
    step_t = softplus(pre_step)
    sig_t = 1.0 / (1.0 + jnp.exp(-pre_step))
    ratio_t = jnp.where(step_t > 0.0, sig_t / step_t, 1.0)
    gate_t = silu(table_z)
    table_vs = jnp.concatenate([table_v, table_s], axis=1)
    taps = jnp.concatenate([cv_ref[...], cs_ref[...]], axis=1)
    none2 = jnp.zeros((4, 2 * heads), F32)
    rest = jnp.zeros((4, 128 - 3 * heads), F32)
    tail = jnp.concatenate(
        [
            gate_t,
            step_t, step_t, -rate_row * step_t, rest,
            none2, sig_t, rest,
            none2, ratio_t, rest,
        ],
        axis=1,
    )
    parts = []
    for k in range(CONV):
        last = tail if k == CONV - 1 else jnp.zeros_like(tail)
        parts.append(jnp.concatenate([table_vs * taps[k : k + 1], last], axis=1))
    per_tap = jnp.concatenate(parts, axis=0)
    p_hi = per_tap.astype(BF16)
    p_rest = per_tap - p_hi.astype(F32)
    p_mid = p_rest.astype(BF16)
    p_low = (p_rest - p_mid.astype(F32)).astype(BF16)
    per_tap3 = jnp.concatenate([p_hi, p_mid, p_low], axis=0)
    place_cols = width + inner

    column = iota((256, 48), 1) % 16
    index, tap = iota((256, 48), 0), column // 4
    digit = lax.shift_right_logical(index & 63, jnp.maximum(2 * (2 - tap), 0)) & 3
    digit = jnp.where(tap == 3, lax.shift_right_logical(index, 6), digit)
    kmer_hits = (digit == column % 4).astype(F32).astype(BF16)
    kmer_sum = dot(kmer_hits, per_tap3[:, : inner + HEAD])
    kmer_tail = dot(kmer_hits, per_tap3[:, place_cols:])
    kx = silu(kmer_sum[:, :inner])
    kb = silu(kmer_sum[:, inner:])
    kb_slope = silu_slope(kmer_sum[:, inner:])

    tri_in = (iota((own, own), 0) <= iota((own, own), 1)).astype(BF16)
    tri_out = (iota((own, own), 0) >= iota((own, own), 1)).astype(BF16)
    pad4 = jnp.zeros((12, own), BF16)

    def complement(v):
        out = jnp.full(v.shape, -1.0, F32)
        for a in range(4):
            out = jnp.where(v == a, rc[a].astype(F32), out)
        return out

    pair = tok_ref[...].astype(F32)
    mine = jnp.concatenate([pair[0:1], pair[1:2]], axis=1)
    mine_rc = complement(mine)
    letters = iota((4, own), 0).astype(F32)
    own_f = (jnp.broadcast_to(mine, (4, own)) == letters).astype(F32)
    own_r = (jnp.broadcast_to(mine_rc, (4, own)) == letters).astype(F32)
    n_f = dot(jnp.concatenate([own_f.astype(BF16), pad4], axis=0), tri_in)
    n_r = dot(jnp.concatenate([own_r.astype(BF16), pad4], axis=0), tri_out)

    def blend(weights, table, h):
        return sum(weights[a : a + 1] * table[a : a + 1, h : h + 1] for a in range(4))

    cum_rows, sig_rows, step_rows, ratio_rows = [], [], [], []
    for counted, hit in ((n_f, own_f), (n_r, own_r)):
        for h in range(heads):
            cum_rows.append(-(rate_row[:, h : h + 1] * blend(counted, step_t, h)))
            sig_rows.append(blend(counted, sig_t, h))
            step_rows.append(blend(hit, step_t, h))
            ratio_rows.append(blend(hit, ratio_t, h))
    cum8 = jnp.concatenate(cum_rows, axis=0)
    both = split(jnp.concatenate([cum8] + sig_rows, axis=0))
    side = jnp.concatenate([both[0], both[1]], axis=0)
    side = jnp.concatenate([side, side], axis=1)
    columns = jnp.transpose(
        jnp.concatenate([cum8, jnp.zeros((128 - 2 * heads, own), F32)], axis=0)
    )
    for n in range(2 * heads):
        if n < heads:
            causal = iota((own, own), 0) >= iota((own, own), 1)
        else:
            causal = iota((own, own), 0) <= iota((own, own), 1)
        cum_c = jnp.broadcast_to(columns[:, n : n + 1], (own, 128))
        for half in range(own // 128):
            at = slice(half * 128, half * 128 + 128)
            decay_ref[n, :, at] = (
                jnp.where(causal[:, at], jnp.exp(cum_c - cum_rows[n][:, at]), 0.0)
                * step_rows[n][:, at]
            )
        part = slice((n % heads) * HEAD, (n % heads + 1) * HEAD)
        grow_ref[n // heads, :, part] = jnp.exp(cum_c)
    loads[14].wait()
    gain = hg_ref[...]
    dg_ref[...] = cot_ref[...].astype(F32) * (gain * loss_scale)

    if links is not None:
        links.take_tokens(tok_ref, (1, blocks - 1))
    earlier = held[lax.rem(me + blocks - 1, blocks)].astype(F32)[1:2]
    later = held[lax.rem(me + 1, blocks)].astype(F32)[0:1]
    earlier = jnp.where(me > 0, earlier, -1.0)
    later = jnp.where(me < blocks - 1, later, -1.0)
    line = jnp.concatenate([earlier, mine, later], axis=1)
    line = jnp.broadcast_to(line, (8, line.shape[1]))
    line_rc = complement(line)
    letters8 = iota((8, own), 0).astype(F32)
    f_hits, r_hits = [], []
    for k in range(CONV):
        d = CONV - 1 - k
        f_line = pltpu.roll(line, d, 1) if d else line
        r_line = pltpu.roll(line_rc, line.shape[1] - d, 1) if d else line_rc
        f_hits.append((f_line[:, 128 : 128 + own] == letters8)[0:4].astype(F32))
        r_hits.append((r_line[:, 128 : 128 + own] == letters8)[0:4].astype(F32))
    hits_t = [jnp.concatenate(f_hits, axis=0), jnp.concatenate(r_hits, axis=0)]
    slopes, c_parts, ct_parts, b_parts = [], [], [], []
    for strand in range(2):
        hits = jnp.concatenate([hits_t[strand]] * 3, axis=0).astype(BF16)
        summed = dot(hits, per_tap3[:, :place_cols], 0, 0)
        gate_ref[strand] = summed[:, width:]
        states = silu(summed[:, inner:width])
        slopes.append(silu_slope(summed[:, inner:width]))
        b_s = split(states[:, :HEAD])
        c_s = split(states[:, HEAD:])
        b_parts.append(b_s)
        c_parts.append(c_s)
        ct_parts.append(split(jnp.transpose(states[:, HEAD:])))
        scores = dot(lhs3(c_s), rhs3(b_s, 1), 1, 1)
        score_ref[strand] = scores
        for h in range(heads):
            part = slice(h * HEAD, (h + 1) * HEAD)
            x_h = silu(summed[:, part])
            x_s = split(x_h)
            xh_ref[strand, :, part] = x_s[0]
            xl_ref[strand, :, part] = x_s[1]
            mixing = split(scores * decay_ref[strand * heads + h])
            y_ref[strand, :, part] = dot(lhs3(mixing), rhs3(x_s)) + skip[h] * x_h

    if links is not None:
        links.take_tokens(tok_ref, range(2, blocks - 1))
    for r in range(blocks):
        kmer_ref[2 * r : 2 * r + 2, :] = held[r].astype(F32)
    tok = kmer_ref[...]
    comp = complement(tok)
    f_shift, r_shift = [tok], [comp]
    for _ in range(CONV - 1):
        f_shift.append(back_one(f_shift[-1], -1.0))
        r_shift.append(ahead_one(r_shift[-1], -1.0))

    row = iota(tok.shape, 0)
    position = row * 128 + iota(tok.shape, 1)
    before = row < 2 * me
    outside = before | (row >= 2 * me + 2)
    kmer_f = f_shift[1] + 4.0 * f_shift[2] + 16.0 * f_shift[3]
    kmer_r = r_shift[1] + 4.0 * r_shift[2] + 16.0 * r_shift[3]
    kmer = jnp.where(before, kmer_f, kmer_r)
    edge = (before & (position < CONV - 1)) | (position >= chunks * 128 - (CONV - 1))
    kmer_ref[...] = jnp.where(edge & outside, -1.0, kmer)
    mixed = jnp.where(outside, jnp.where(before, tok, comp), -1.0)
    last_ref[...] = mixed
    tri = (iota((128, 128), 0) <= iota((128, 128), 1)).astype(BF16)
    ones = jnp.ones((128, 128), BF16)
    strict = (iota((chunks, chunks), 1) < iota((chunks, chunks), 0)).astype(BF16)
    counts = []
    for a in range(4):
        hit = (mixed == a).astype(F32)
        hit16 = hit.astype(BF16)
        within = dot(hit16, tri)
        offset = dot(strict, dot(hit16, ones).astype(BF16))
        total_f = jnp.sum(jnp.where(before, hit, 0.0), keepdims=True)
        inclusive = within + offset - total_f
        counts.append(jnp.where(before, -inclusive, inclusive - hit))
    for h in range(heads):
        steps_sum = sum(counts[a] * step_t[a : a + 1, h : h + 1] for a in range(4))
        sig_sum = sum(counts[a] * sig_t[a : a + 1, h : h + 1] for a in range(4))
        exponent = -(rate_row[:, h : h + 1] * steps_sum)
        decay = jnp.where(outside, jnp.exp(exponent), 0.0)
        for q, value in enumerate((decay, decay * exponent, decay * sig_sum)):
            base = (q * heads + h) * chunks
            rows_ref[base : base + chunks, :] = value
    for q in range(3 * heads, 16):
        rows_ref[q * chunks : (q + 1) * chunks, :] = jnp.zeros((chunks, 128), F32)

    first_id = iota((64, 128), 0).astype(F32).astype(BF16)
    one16, zero16 = jnp.ones((64, 128), BF16), jnp.zeros((64, 128), BF16)
    nothing = jnp.zeros((32, 128), BF16)

    def load_rows(chunk):
        return rows_ref[pl.ds(chunk, 16, stride=chunks), :]

    acc_f = jnp.zeros((64, 128), F32)
    acc_r = jnp.zeros((64, 128), F32)
    for block in range(blocks):
        hits, weights = [], []
        for chunk in (2 * block, 2 * block + 1):
            w = jnp.concatenate(split(load_rows(chunk)), axis=0)
            final = jnp.broadcast_to(last_ref[chunk : chunk + 1, :], (32, 128)).astype(BF16)
            weights.append(
                jnp.concatenate([jnp.where(final == a, w, nothing) for a in range(4)], axis=0)
            )
            ids = jnp.broadcast_to(kmer_ref[chunk : chunk + 1, :], (64, 128)).astype(BF16)
            hits.append(jnp.where(ids == first_id, one16, zero16))
        found = dot(jnp.concatenate(hits, axis=1), jnp.concatenate(weights, axis=1), 1, 1)
        acc_f = acc_f + jnp.where(block < me, found, 0.0)
        acc_r = acc_r + jnp.where(block > me, found, 0.0)
    lane = iota((16, 128), 1)
    e_f = split(jnp.where(lane < CONV - 1, load_rows(0), 0.0))
    e_r = split(jnp.where(lane >= 128 - (CONV - 1), load_rows(chunks - 1), 0.0))
    pick_row = iota((16, 128), 0)
    pick = (lane == jnp.where(pick_row < 8, pick_row, pick_row + 112)).astype(BF16)

    def by_row(acc, ends):
        parts = [acc] + [pltpu.roll(acc, 128 - 32 * a, 1) for a in range(1, 4)]
        ends = jnp.concatenate([ends[0], ends[1], jnp.zeros((96, 128), BF16)], axis=0)
        joined = jnp.concatenate(parts + [dot(pick, ends, 1, 1)], axis=0)
        return joined + pltpu.roll(joined, 128 - 16, 1)

    joined = (by_row(acc_f, e_f), by_row(acc_r, e_r))

    end_hits = []
    for k in range(CONV):
        d = CONV - 1 - k
        ends = jnp.where(
            iota((1, 128), 1) < 64, f_shift[d][0:1, :], r_shift[d][chunks - 1 : chunks, :]
        )
        end_hits.append(
            (jnp.broadcast_to(ends, (4, 128)) == iota((4, 128), 0).astype(F32)).astype(F32)
        )
    end_hits = jnp.concatenate(end_hits, axis=0).astype(BF16)
    end_pick = dot(end_hits, pick, 1, 1)
    end3 = jnp.concatenate([end_pick] * 3, axis=0).astype(BF16)
    end_sum = dot(end3, per_tap3, 0, 0)
    kx = jnp.concatenate([kx, silu(end_sum[:, :inner])], axis=0)
    kb = jnp.concatenate([kb, silu(end_sum[:, inner : inner + HEAD])], axis=0)
    kb_slope = jnp.concatenate([kb_slope, silu_slope(end_sum[:, inner : inner + HEAD])], axis=0)
    k_tail = jnp.concatenate([kmer_tail, end_sum[:, place_cols:]], axis=0)
    table_rows = kx.shape[0]

    lanes = iota((1, 128), 1)
    lane_rate = jnp.zeros((1, 128), F32)
    for h in range(heads):
        lane_rate = jnp.where(lanes == 2 * heads + h, -rate_row[:, h : h + 1], lane_rate)
    lane_one = jnp.where((lanes >= heads) & (lanes < 2 * heads), 1.0, lane_rate)
    weights, ratios, kxw_parts = [], [], []
    for strand in range(2):
        source = joined[strand]
        w = k_tail[:, 0:128] * source
        e4, e8 = pltpu.roll(source, heads, 1), pltpu.roll(source, 2 * heads, 1)
        decay = jnp.where((lanes >= heads) & (lanes < 2 * heads), e4, e8)
        kept = (decay > 0.0) & (lanes >= heads) & (lanes < 3 * heads)
        ratio = jnp.where(
            kept, lane_one * source / jnp.where(kept, decay, 1.0) + k_tail[:, 256:384], 0.0
        )
        ratio = jnp.concatenate(
            [ratio, jnp.zeros((384 - table_rows, 128), F32)], axis=0
        )
        ratio = split(jnp.transpose(ratio)[0:16, :table_rows])
        ratios.append(jnp.concatenate([ratio[0], ratio[1]], axis=0))
        kxw_parts.append(
            split(
                jnp.concatenate(
                    [
                        kx[:, h * HEAD : (h + 1) * HEAD]
                        * jnp.broadcast_to(w[:, h : h + 1], (table_rows, HEAD))
                        for h in range(heads)
                    ],
                    axis=1,
                )
            )
        )
    kb_t = jnp.concatenate([kb, jnp.zeros((384 - table_rows, HEAD), F32)], axis=0)
    kb_t = split(jnp.transpose(kb_t)[:, :table_rows])

    d_kb = [jnp.zeros(kb.shape, F32)]
    rate_grads = [jnp.zeros((1, 128), F32)] * heads
    bias_grads = [jnp.zeros((1, 128), F32)] * heads
    tap_sums = [jnp.zeros((16, 2 * HEAD), F32)]
    starts, d_scores, d_starts = [], [None, None], [None, None]
    for strand in range(2):
        kxw = kxw_parts[strand]
        start = dot(kb_t[0], kxw[0]) + (dot(kb_t[0], kxw[1]) + dot(kb_t[1], kxw[0]))
        starts.append(split(start))
        car_ref[strand] = dot(lhs3(c_parts[strand]), rhs3(starts[strand]))

    def head_pass(strand, h):
        n = strand * heads + h
        part = slice(h * HEAD, (h + 1) * HEAD)
        grow = grow_ref[strand, :, part]
        from_start = grow * car_ref[strand, :, part]
        gate = gate_ref[strand, :, part]
        gated = (y_ref[strand, :, part] + from_start) * gate
        inv = lax.rsqrt(jnp.mean(gated * gated, axis=1, keepdims=True) + EPS)
        normal = gated * inv
        out = normal * gain[:, part]
        if strand == 0:
            y_ref[0, :, part] = out
        else:
            enc_ref[:, part] = (y_ref[0, :, part] + out).astype(BF16)
        d_normal = dg_ref[:, part]
        d_y = d_normal - normal * jnp.mean(normal * d_normal, axis=1, keepdims=True)
        d_y = (d_y * inv) * gate
        x_s = (xh_ref[strand, :, part], xl_ref[strand, :, part])
        mixed_grad = dot(lhs3(split(d_y)), rhs3(x_s, 1), 1, 1) * decay_ref[n]
        d_scores[strand] = mixed_grad if h == 0 else d_scores[strand] + mixed_grad
        weighted = mixed_grad * score_ref[strand]
        wsum = split(fold(weighted) + d_y * from_start)
        moved = dot(side, jnp.concatenate([wsum[0], wsum[1]], axis=0))
        col_sum = jnp.sum(weighted, axis=0, keepdims=True)
        grown = split(d_y * grow)
        gh_ref[strand, :, part] = grown[0]
        gl_ref[strand, :, part] = grown[1]
        rate = rate_row[:, h : h + 1]
        rows = 2 * heads
        rate_grads[h] = (
            rate_grads[h]
            + (moved[n : n + 1] + moved[2 * rows + n : 2 * rows + n + 1])
            - fold(col_sum * cum_rows[n])
        )
        bias_grads[h] = (
            bias_grads[h]
            + fold(col_sum * (rate * sig_rows[n] + ratio_rows[n]))
            - rate * (moved[rows + n : rows + n + 1] + moved[3 * rows + n : 3 * rows + n + 1])
        )

    def state_pass(strand):
        grown = (gh_ref[strand], gl_ref[strand])
        d_starts[strand] = split(dot(lhs3(ct_parts[strand]), rhs3(grown)))

    def table_pass(strand, h):
        part = slice(h * HEAD, (h + 1) * HEAD)
        d_start_h = (d_starts[strand][0][:, part], d_starts[strand][1][:, part])
        pulled = dot(
            lhs3((kxw_parts[strand][0][:, part], kxw_parts[strand][1][:, part])), rhs3(d_start_h, 1), 1, 1
        )
        d_kb[0] = d_kb[0] + pulled
        t = split(pulled * kb)
        slope = dot(ratios[strand], t[0]) + dot(ratios[strand], t[1])
        slope = slope[0:16] + slope[16:32]
        rate_grads[h] = rate_grads[h] + slope[heads + h : heads + h + 1]
        bias_grads[h] = bias_grads[h] + slope[2 * heads + h : 2 * heads + h + 1]

    def local_pass(strand):
        d_scores_s = split(d_scores[strand])
        d_c = dot(lhs3(d_scores_s), rhs3(b_parts[strand])) + dot(lhs3((gh_ref[strand], gl_ref[strand])), rhs3(starts[strand], 1), 1, 1)
        d_b = dot(lhs3(split(jnp.transpose(d_scores[strand]))), rhs3(c_parts[strand]))
        d_sum = split(jnp.concatenate([d_b, d_c], axis=1) * slopes[strand])
        hits = hits_t[strand].astype(BF16)
        tap_sums[0] = tap_sums[0] + dot(
            jnp.concatenate([hits, hits], axis=1), jnp.concatenate([d_sum[0], d_sum[1]], axis=0)
        )

    for h in range(heads):
        head_pass(0, h)
    state_pass(0)
    for h in range(heads):
        head_pass(1, h)
        table_pass(0, h)
    leave = pltpu.make_async_copy(enc_ref, enc_hbm, load_sem.at[len(loads)])
    leave.start()
    local_pass(0)
    state_pass(1)
    for h in range(heads):
        table_pass(1, h)
    local_pass(1)
    d_kb, tap_sums = d_kb[0], tap_sums[0]
    d_kb = split(d_kb * kb_slope)
    b_sums = dot(kmer_hits[:, 0:16], d_kb[0][0:256], 0, 0)
    b_sums = b_sums + dot(kmer_hits[:, 0:16], d_kb[1][0:256], 0, 0)
    end_pick = end_pick.astype(BF16)
    b_sums = b_sums + dot(end_pick, d_kb[0][256:]) + dot(end_pick, d_kb[1][256:])
    tap_sums = tap_sums + jnp.concatenate([b_sums, jnp.zeros_like(b_sums)], axis=1)
    conv_rows = []
    for k in range(CONV):
        conv_rows.append(
            jnp.sum(tap_sums[4 * k : 4 * k + 4] * table_s, axis=0, keepdims=True)
        )
    sums = jnp.sum(jnp.concatenate(rate_grads + bias_grads, axis=0), axis=1, keepdims=True)
    lane8 = iota((8, 128), 1)
    row8 = iota((8, 128), 0)
    last = jnp.zeros((8, 128), F32)
    head_total = 8 * heads
    for h in range(heads):
        at = slot * heads + h
        last = jnp.where((row8 == 0) & (lane8 == at), sums[h : h + 1], last)
        last = jnp.where(
            (row8 == 0) & (lane8 == head_total + at), sums[heads + h : heads + h + 1], last
        )
    conv = jnp.concatenate(conv_rows, axis=0)
    value = jnp.concatenate([conv[:, :128], conv[:, 128:], last[0:1]], axis=0)
    if links is not None:
        value = links.reduce(value)
    pay_ref[...] = value
    leave.wait()
    if links is not None:
        links.drain()


def layer(args, place, loss_scale, everyone=None, interpret=False):
    (tokens, rc_map, embedding, norm_gain, w_values, w_gates, w_states, w_steps, conv_values,
     conv_states, step_bias, log_rate, skip_gain, head_gain, cotangent) = args
    own, inner = cotangent.shape
    blocks = SIZES["x"] * SIZES["z"]
    chunks = 2 * blocks
    hbm = pl.BlockSpec(memory_space=pl.ANY)
    inputs = [
        tokens, rc_map, step_bias, log_rate, skip_gain, embedding, norm_gain.reshape(1, -1),
        conv_values, conv_states, head_gain.reshape(1, -1), w_states, w_steps.T, w_values, w_gates,
        cotangent,
    ]
    count = len(inputs)
    stores = [
        (pltpu.SMEM if 1 <= n <= 4 else pltpu.VMEM)(a.shape, a.dtype) for n, a in enumerate(inputs)
    ]
    scratch = [
        pltpu.VMEM((chunks, 128), F32),
        pltpu.VMEM((chunks, 128), F32),
        pltpu.VMEM((16 * chunks, 128), F32),
        pltpu.VMEM((8, own, own), F32),
        pltpu.SemaphoreType.DMA((count + 1,)),
        pltpu.VMEM((2, own, inner), BF16),
        pltpu.VMEM((2, own, inner), BF16),
        pltpu.VMEM((2, own, inner), F32),
        pltpu.VMEM((2, own, inner), F32),
        pltpu.VMEM((2, own, inner), F32),
        pltpu.VMEM((own, inner), F32),
        pltpu.VMEM((2, own, own), F32),
        pltpu.VMEM((2, own, inner), BF16),
        pltpu.VMEM((2, own, inner), BF16),
        pltpu.VMEM((2, own, inner), F32),
        pltpu.VMEM((own, inner), BF16),
    ]
    slots = SIZES["c"] + SIZES["x"] * SIZES["y"] + SIZES["z"]
    remote = [
        pltpu.VMEM((blocks, 2, 128), jnp.int32),
        pltpu.VMEM((slots, 9, 128), F32),
        pltpu.VMEM((3, 9, 128), F32),
        pltpu.SemaphoreType.DMA((blocks,)),
        pltpu.SemaphoreType.DMA((blocks,)),
        pltpu.SemaphoreType.DMA((slots,)),
        pltpu.SemaphoreType.DMA((slots,)),
    ]
    shapes = (
        jax.ShapeDtypeStruct((own, inner), BF16),
        jax.ShapeDtypeStruct((9, 128), F32),
    )
    alone = everyone is not None

    def body(*refs):
        refs = list(refs)
        sources, refs = refs[:count], refs[count:]
        if alone:
            links, held, refs = None, refs[0], refs[1:]
            out, refs = refs[:2], refs[2:]
        else:
            out, refs = refs[:2], refs[2:]
            links, held, refs = Links(refs[:7]), refs[0], refs[7:]
        layer_kernel(
            place, links, sources, *out, held, refs[:count], *refs[count:], loss_scale=loss_scale
        )

    if alone:
        params = pltpu.CompilerParams(vmem_limit_bytes=60 * 1024 * 1024)
    else:
        params = pltpu.CompilerParams(
            vmem_limit_bytes=60 * 1024 * 1024, collective_id=0, has_side_effects=True
        )
    return pl.pallas_call(
        body,
        out_shape=shapes,
        in_specs=[hbm] * count + [VM] * alone,
        out_specs=(hbm, VM),
        scratch_shapes=([] if alone else remote) + stores + scratch,
        compiler_params=params,
        interpret=interpret,
        name="layer",
    )(*inputs, *([everyone] if alone else []))


def emit_kernel(enc_ref, pay_ref, out_ref, rate_ref, bias_ref, conv_ref):
    heads = rate_ref.shape[1]
    out_ref[...] = enc_ref[...]
    rate_ref[...] = pay_ref[8:9, 0:heads]
    bias_ref[...] = pay_ref[8:9, heads : 2 * heads]
    conv_ref[...] = jnp.concatenate([pay_ref[0:4, :], pay_ref[4:8, :]], axis=1)


def emit(encoded, pay, heads):
    return pl.pallas_call(
        emit_kernel,
        out_shape=(
            jax.ShapeDtypeStruct(encoded.shape, BF16),
            jax.ShapeDtypeStruct((1, heads), F32),
            jax.ShapeDtypeStruct((1, heads), F32),
            jax.ShapeDtypeStruct((4, 256), F32),
        ),
        in_specs=[VM] * 2,
        out_specs=(VM,) * 4,
        name="emit",
    )(encoded, pay)


def solution(mesh):
    count = mesh.shape["ctx"]

    def on_device(*args):
        own = args[-1].shape[0]
        loss_scale = 1.0 / math.sqrt(own * count * HEAD)

        def place():
            return lax.axis_index("ctx"), lax.axis_index("tp")

        heads = args[11].shape[0] * mesh.shape["tp"]
        encoded, pay = layer((args[0].reshape(2, 128),) + args[1:], place, loss_scale)
        encoded, rate, bias, conv = emit(encoded, pay, heads)
        return encoded, rate.reshape(-1), bias.reshape(-1), conv

    tp = P("tp")
    cols = P(None, "tp")
    in_specs = (
        P("ctx"), P(), P(), P(), cols, cols, P(), cols, cols, P(), tp, tp, tp, tp, P("ctx", "tp"),
    )
    return jax.shard_map(
        on_device, mesh=mesh, in_specs=in_specs,
        out_specs=(P("ctx", "tp"), P(), P(), P()), check_vma=False,
    )
```

time: 46 us -> 39.9 us (0.87)
  Pallas kernels: 45.2 us -> 39.1 us
    pallas_call x1, Pallas kernels: 43.5 us -> 37.4 us  [layer(): pl.pallas_call(body, out_shape=shapes, in_specs=[hbm] * count + [VM] * al...]
where the time goes in v3:
time: 39.9 us; the launch traced here: 39.8 us
  Pallas kernels  39.1 us (98%)
  between operations  0.65 us (2%)
    pallas_call x1, Pallas kernels, layer(): pl.pallas_call(body, out_shape=shapes, in_specs=[hbm] * count + [VM] * al...  37.4 us
    pallas_call x1, Pallas kernels, emit(): pl.pallas_call(emit_kernel, out_shape=(jax.ShapeDtypeStruct(encoded.shape...  1.68 us

profile of v3, /device:TPU:1, one launch (start us, length us, event | category | flops | bytes accessed | tf_op | source)
XLA Modules:
  0.0 39.8 jit_solution(4780016664783804614)
XLA Ops:
  0.6 37.4 %layer.1 = (bf16[256,512]{1,0:T(8,128)(2,1)}, f32[9,128]{1,0:T(8,128)}) custom-call(s32[2,128]{1,0:T(2,128)} %bitcast.9, s32[4]{0:T(128)} %refs_1_.1, f32[4]{0:T(128)} %refs_2_.1, f32[4]{0:T(128)} %refs_3_.1, f32[4]{0:T(128)} %refs_4_.1, bf16[4,2048]{1,0:T(4,128)(2,1)} %refs_5_.1, f32[1,2048]{1,0:T(1,128)} %bitcast.7, f32[4,512]{1,0:T(4,128)} %refs_7_.1, ...), custom_call_target="tpu_custom_call" | custom-call | tf_op jit(solution)/shard_map/layer/pallas_call | solution.py:707
  38.1 1.7 %emit.1 = (bf16[256,512]{1,0:T(8,128)(2,1)}, f32[1,32]{1,0:T(1,128)}, f32[1,32]{1,0:T(1,128)}, f32[4,256]{1,0:T(4,128)}) custom-call(bf16[256,512]{1,0:T(8,128)(2,1)} %get-tuple-element.10.enc_ref, f32[9,128]{1,0:T(8,128)} %get-tuple-element.11.pay_ref), custom_call_target="tpu_custom_call" | custom-call | tf_op jit(solution)/shard_map/emit/pallas_call | solution.py:728

commit v4 on v3

--- a/solution.py
+++ b/solution.py
@@ -89,8 +89,8 @@
 
 class Links:
     def __init__(self, refs):
-        (self.held, self.slots, self.sent, self.tok_send, self.tok_recv, self.sum_send,
-         self.sum_recv) = refs
+        (self.held, self.near, self.slots, self.sent, self.tok_send, self.tok_recv,
+         self.sum_send, self.sum_recv) = refs
         ctx, tp = lax.axis_index("ctx"), lax.axis_index("tp")
         self.ctx = ctx
         self.here = {
@@ -111,53 +111,72 @@
             "ctx": there["x"] * SIZES["z"] + there["z"], "tp": there["y"] * SIZES["c"] + there["c"]
         }
 
+    def beside(self, d):
+        count = SIZES["x"] * SIZES["z"]
+        return {"ctx": lax.rem(self.ctx + d % count, count)}
+
     def greet(self):
         barrier = pltpu.get_barrier_semaphore()
-        self.greeted = 0
-        plane = [step for step in offsets("xy") if step[1]]
-        for axes, steps in (("xz", offsets("xz")), ("xy", plane), ("c", offsets("c"))):
-            for step in steps:
-                device = self.device(self.moved(axes, step))
-                pl.semaphore_signal(barrier, inc=1, device_id=device, device_id_type=MESH)
-                self.greeted += 1
+        devices = [self.device(self.moved("z", step)) for step in offsets("z")]
+        devices += [self.device(self.moved("x", step)) for step in offsets("x")]
+        devices += [self.beside(1), self.beside(-1)]
+        devices += [self.device(self.moved("xy", step)) for step in offsets("xy") if step[1]]
+        devices += [self.device(self.moved("c", step)) for step in offsets("c")]
+        for device in devices:
+            pl.semaphore_signal(barrier, inc=1, device_id=device, device_id_type=MESH)
+        self.greeted = len(devices)
 
     def met(self):
         pl.semaphore_wait(pltpu.get_barrier_semaphore(), self.greeted)
 
+    def token_copy(self, source, target, number, arrives, device):
+        return pltpu.make_async_remote_copy(
+            src_ref=source, dst_ref=target, send_sem=self.tok_send.at[number],
+            recv_sem=self.tok_recv.at[arrives], device_id=device, device_id_type=MESH,
+        )
+
+    def send(self, copy):
+        copy.start()
+        self.drains.append(copy)
+
     def send_tokens(self, tok_ref):
-        for k, step in enumerate(offsets("xz")):
-            copy = pltpu.make_async_remote_copy(
-                src_ref=tok_ref,
-                dst_ref=self.held.at[self.ctx],
-                send_sem=self.tok_send.at[k],
-                recv_sem=self.tok_recv.at[self.ctx],
-                device_id=self.device(self.moved("xz", step)),
-                device_id_type=MESH,
-            )
-            copy.start()
-            self.drains.append(copy)
-        self.held[self.ctx] = tok_ref[...]
-
-    def take_one(self, tok_ref, source):
-        pltpu.make_async_remote_copy(
-            src_ref=tok_ref,
-            dst_ref=self.held.at[source],
-            send_sem=self.tok_send.at[0],
-            recv_sem=self.tok_recv.at[source],
-            device_id={"ctx": source},
-            device_id_type=MESH,
-        ).wait_recv()
-
-    def take_tokens(self, tok_ref, steps):
-        count = self.held.shape[0]
-        for k in steps:
-            self.take_one(tok_ref, lax.rem(self.ctx + k, count))
+        x, z = self.here["x"], self.here["z"]
+        own = self.held.at[z, x]
+        for k, step in enumerate(offsets("x")):
+            self.send(self.token_copy(tok_ref, own, k, x, self.device(self.moved("x", step))))
+        for k, d in ((3, 1), (4, -1)):
+            near = self.near.at[k - 3]
+            self.send(self.token_copy(tok_ref, near, k, 9 + k, self.beside(d)))
+        self.held[z, x] = tok_ref[...]
+
+    def pass_tokens(self, tok_ref):
+        x, z = self.here["x"], self.here["z"]
+        for step in reversed(offsets("x")):
+            there = self.moved("x", step)
+            self.token_copy(
+                tok_ref, self.held.at[z, there["x"]], 0, there["x"], self.device(there)
+            ).wait_recv()
+        row = self.held.at[z]
+        for k, step in enumerate(offsets("z")):
+            there = self.moved("z", step)
+            self.send(self.token_copy(row, row, 5 + k, 4 + z, self.device(there)))
+
+    def take_beside(self, tok_ref):
+        for k, d in ((3, 1), (4, -1)):
+            self.token_copy(tok_ref, self.near.at[k - 3], k, 9 + k, self.beside(d)).wait_recv()
+
+    def take_tokens(self):
+        for step in reversed(offsets("z")):
+            there = self.moved("z", step)
+            row = self.held.at[there["z"]]
+            self.token_copy(row, row, 5, 4 + there["z"], self.device(there)).wait_recv()
 
     def reduce(self, value):
         base = 0
         for number, axes in enumerate(("c", "xy", "z")):
             self.sent[number] = value
             steps = offsets(axes)
+            sending = []
 
             def slot(there):
                 place = 0
@@ -176,9 +195,10 @@
                 )
 
             for k, step in enumerate(steps):
-                sending = copy(k, self.moved(axes, step), slot(self.here))
-                sending.start()
-                self.drains.append(sending)
+                sending.append(copy(k, self.moved(axes, step), slot(self.here)))
+                sending[-1].start()
+            self.drain()
+            self.drains = sending
             self.slots[slot(self.here)] = value
             for step in reversed(steps):
                 there = self.moved(axes, step)
@@ -196,7 +216,7 @@
 
 def layer_kernel(
     place, links, sources, enc_hbm, pay_ref, held, stores, kmer_ref, last_ref, rows_ref, decay_ref, load_sem,
-    xh_ref, xl_ref, y_ref, gate_ref, grow_ref, dg_ref, score_ref, gh_ref, gl_ref, car_ref, enc_ref,
+    xh_ref, xl_ref, y_ref, gate_ref, grow_ref, dg_ref, score_ref, gh_ref, gl_ref, car_ref, enc_ref, kxw_ref,
     *, loss_scale,
 ):
     if links is not None:
@@ -210,7 +230,7 @@
     (tok_ref, rc, bias, log_rate, skip, emb_ref, ng_ref, cv_ref, cs_ref, hg_ref, ws_ref, wst_ref,
      wv_ref, wg_ref, cot_ref) = stores
     me, slot = place()
-    blocks = held.shape[0]
+    blocks = SIZES["x"] * SIZES["z"]
     chunks = 2 * blocks
     inner = cv_ref.shape[1]
     heads = inner // HEAD
@@ -336,9 +356,15 @@
     dg_ref[...] = cot_ref[...].astype(F32) * (gain * loss_scale)
 
     if links is not None:
-        links.take_tokens(tok_ref, (1, blocks - 1))
-    earlier = held[lax.rem(me + blocks - 1, blocks)].astype(F32)[1:2]
-    later = held[lax.rem(me + 1, blocks)].astype(F32)[0:1]
+        links.pass_tokens(tok_ref)
+        links.take_beside(tok_ref)
+        earlier, later = links.near[0], links.near[1]
+    else:
+        earlier, later = (
+            held[lax.rem(there, SIZES["z"]), there // SIZES["z"]]
+            for there in (lax.rem(me + blocks - 1, blocks), lax.rem(me + 1, blocks))
+        )
+    earlier, later = earlier.astype(F32)[1:2], later.astype(F32)[0:1]
     earlier = jnp.where(me > 0, earlier, -1.0)
     later = jnp.where(me < blocks - 1, later, -1.0)
     line = jnp.concatenate([earlier, mine, later], axis=1)
@@ -377,9 +403,9 @@
             y_ref[strand, :, part] = dot(lhs3(mixing), rhs3(x_s)) + skip[h] * x_h
 
     if links is not None:
-        links.take_tokens(tok_ref, range(2, blocks - 1))
+        links.take_tokens()
     for r in range(blocks):
-        kmer_ref[2 * r : 2 * r + 2, :] = held[r].astype(F32)
+        kmer_ref[2 * r : 2 * r + 2, :] = held[r % SIZES["z"], r // SIZES["z"]].astype(F32)
     tok = kmer_ref[...]
     comp = complement(tok)
     f_shift, r_shift = [tok], [comp]
@@ -496,18 +522,12 @@
         )
         ratio = split(jnp.transpose(ratio)[0:16, :table_rows])
         ratios.append(jnp.concatenate([ratio[0], ratio[1]], axis=0))
-        kxw_parts.append(
-            split(
-                jnp.concatenate(
-                    [
-                        kx[:, h * HEAD : (h + 1) * HEAD]
-                        * jnp.broadcast_to(w[:, h : h + 1], (table_rows, HEAD))
-                        for h in range(heads)
-                    ],
-                    axis=1,
-                )
+        for h in range(heads):
+            part = slice(h * HEAD, (h + 1) * HEAD)
+            kxw_ref[strand, :, part] = kx[:, part] * jnp.broadcast_to(
+                w[:, h : h + 1], (table_rows, HEAD)
             )
-        )
+        kxw_parts.append(split(kxw_ref[strand]))
     kb_t = jnp.concatenate([kb, jnp.zeros((384 - table_rows, HEAD), F32)], axis=0)
     kb_t = split(jnp.transpose(kb_t)[:, :table_rows])
 
@@ -566,18 +586,16 @@
         grown = (gh_ref[strand], gl_ref[strand])
         d_starts[strand] = split(dot(lhs3(ct_parts[strand]), rhs3(grown)))
 
-    def table_pass(strand, h):
-        part = slice(h * HEAD, (h + 1) * HEAD)
-        d_start_h = (d_starts[strand][0][:, part], d_starts[strand][1][:, part])
-        pulled = dot(
-            lhs3((kxw_parts[strand][0][:, part], kxw_parts[strand][1][:, part])), rhs3(d_start_h, 1), 1, 1
-        )
-        d_kb[0] = d_kb[0] + pulled
-        t = split(pulled * kb)
-        slope = dot(ratios[strand], t[0]) + dot(ratios[strand], t[1])
+    def table_pass(strand):
+        kxw, d_start = kxw_parts[strand], d_starts[strand]
+        d_kb[0] = d_kb[0] + dot(lhs3(kxw), rhs3(d_start, 1), 1, 1)
+        met = split(dot(lhs3(split(kb)), rhs3(d_start)) * kxw_ref[strand])
+        slope = dot(ratios[strand], met[0]) + dot(ratios[strand], met[1])
         slope = slope[0:16] + slope[16:32]
-        rate_grads[h] = rate_grads[h] + slope[heads + h : heads + h + 1]
-        bias_grads[h] = bias_grads[h] + slope[2 * heads + h : 2 * heads + h + 1]
+        for h in range(heads):
+            part = slice(h * HEAD, (h + 1) * HEAD)
+            rate_grads[h] = rate_grads[h] + slope[heads + h : heads + h + 1, part]
+            bias_grads[h] = bias_grads[h] + slope[2 * heads + h : 2 * heads + h + 1, part]
 
     def local_pass(strand):
         d_scores_s = split(d_scores[strand])
@@ -594,13 +612,13 @@
     state_pass(0)
     for h in range(heads):
         head_pass(1, h)
-        table_pass(0, h)
+        if h == 0:
+            table_pass(0)
     leave = pltpu.make_async_copy(enc_ref, enc_hbm, load_sem.at[len(loads)])
     leave.start()
     local_pass(0)
     state_pass(1)
-    for h in range(heads):
-        table_pass(1, h)
+    table_pass(1)
     local_pass(1)
     d_kb, tap_sums = d_kb[0], tap_sums[0]
     d_kb = split(d_kb * kb_slope)
@@ -668,14 +686,16 @@
         pltpu.VMEM((2, own, inner), BF16),
         pltpu.VMEM((2, own, inner), F32),
         pltpu.VMEM((own, inner), BF16),
+        pltpu.VMEM((2, 256 + 16, inner), F32),
     ]
     slots = SIZES["c"] + SIZES["x"] * SIZES["y"] + SIZES["z"]
     remote = [
-        pltpu.VMEM((blocks, 2, 128), jnp.int32),
+        pltpu.VMEM((SIZES["z"], SIZES["x"], 2, 128), jnp.int32),
+        pltpu.VMEM((2, 2, 128), jnp.int32),
         pltpu.VMEM((slots, 9, 128), F32),
         pltpu.VMEM((3, 9, 128), F32),
-        pltpu.SemaphoreType.DMA((blocks,)),
-        pltpu.SemaphoreType.DMA((blocks,)),
+        pltpu.SemaphoreType.DMA((12,)),
+        pltpu.SemaphoreType.DMA((14,)),
         pltpu.SemaphoreType.DMA((slots,)),
         pltpu.SemaphoreType.DMA((slots,)),
     ]
@@ -693,7 +713,7 @@
             out, refs = refs[:2], refs[2:]
         else:
             out, refs = refs[:2], refs[2:]
-            links, held, refs = Links(refs[:7]), refs[0], refs[7:]
+            links, held, refs = Links(refs[:8]), refs[0], refs[8:]
         layer_kernel(
             place, links, sources, *out, held, refs[:count], *refs[count:], loss_scale=loss_scale
         )

time: 39.9 us -> 38.7 us (0.970)
  Pallas kernels: 39.1 us -> 38 us
    pallas_call x1, Pallas kernels: 37.4 us -> 36.3 us  [layer(): pl.pallas_call(body, out_shape=shapes, in_specs=[hbm] * count + [VM] * al...]
where the time goes in v4:
time: 38.7 us; the launch traced here: 38.6 us
  Pallas kernels  38 us (98%)
  between operations  0.65 us (2%)
    pallas_call x1, Pallas kernels, layer(): pl.pallas_call(body, out_shape=shapes, in_specs=[hbm] * count + [VM] * al...  36.3 us
    pallas_call x1, Pallas kernels, emit(): pl.pallas_call(emit_kernel, out_shape=(jax.ShapeDtypeStruct(encoded.shape...  1.68 us

profile of v4, /device:TPU:1, one launch (start us, length us, event | category | flops | bytes accessed | tf_op | source)
XLA Modules:
  0.0 38.6 jit_solution(14964328915391592187)
XLA Ops:
  0.6 36.3 %layer.1 = (bf16[256,512]{1,0:T(8,128)(2,1)}, f32[9,128]{1,0:T(8,128)}) custom-call(s32[2,128]{1,0:T(2,128)} %bitcast.9, s32[4]{0:T(128)} %refs_1_.1, f32[4]{0:T(128)} %refs_2_.1, f32[4]{0:T(128)} %refs_3_.1, f32[4]{0:T(128)} %refs_4_.1, bf16[4,2048]{1,0:T(4,128)(2,1)} %refs_5_.1, f32[1,2048]{1,0:T(1,128)} %bitcast.7, f32[4,512]{1,0:T(4,128)} %refs_7_.1, ...), custom_call_target="tpu_custom_call" | custom-call | tf_op jit(solution)/shard_map/layer/pallas_call | solution.py:727
  36.9 1.7 %emit.1 = (bf16[256,512]{1,0:T(8,128)(2,1)}, f32[1,32]{1,0:T(1,128)}, f32[1,32]{1,0:T(1,128)}, f32[4,256]{1,0:T(4,128)}) custom-call(bf16[256,512]{1,0:T(8,128)(2,1)} %get-tuple-element.10.enc_ref, f32[9,128]{1,0:T(8,128)} %get-tuple-element.11.pay_ref), custom_call_target="tpu_custom_call" | custom-call | tf_op jit(solution)/shard_map/emit/pallas_call | solution.py:748

commit v5 on v4

--- a/solution.py
+++ b/solution.py
@@ -215,8 +215,8 @@
 
 
 def layer_kernel(
-    place, links, sources, enc_hbm, pay_ref, held, stores, kmer_ref, last_ref, rows_ref, decay_ref, load_sem,
-    xh_ref, xl_ref, y_ref, gate_ref, grow_ref, dg_ref, score_ref, gh_ref, gl_ref, car_ref, enc_ref, kxw_ref,
+    place, links, sources, enc_ref, pay_ref, held, stores, kmer_ref, last_ref, rows_ref, decay_ref, load_sem,
+    xh_ref, xl_ref, y_ref, gate_ref, grow_ref, dg_ref, score_ref, gh_ref, gl_ref, car_ref, kxw_ref,
     *, loss_scale,
 ):
     if links is not None:
@@ -614,8 +614,6 @@
         head_pass(1, h)
         if h == 0:
             table_pass(0)
-    leave = pltpu.make_async_copy(enc_ref, enc_hbm, load_sem.at[len(loads)])
-    leave.start()
     local_pass(0)
     state_pass(1)
     table_pass(1)
@@ -648,7 +646,6 @@
     if links is not None:
         value = links.reduce(value)
     pay_ref[...] = value
-    leave.wait()
     if links is not None:
         links.drain()
 
@@ -674,7 +671,7 @@
         pltpu.VMEM((chunks, 128), F32),
         pltpu.VMEM((16 * chunks, 128), F32),
         pltpu.VMEM((8, own, own), F32),
-        pltpu.SemaphoreType.DMA((count + 1,)),
+        pltpu.SemaphoreType.DMA((count,)),
         pltpu.VMEM((2, own, inner), BF16),
         pltpu.VMEM((2, own, inner), BF16),
         pltpu.VMEM((2, own, inner), F32),
@@ -685,7 +682,6 @@
         pltpu.VMEM((2, own, inner), BF16),
         pltpu.VMEM((2, own, inner), BF16),
         pltpu.VMEM((2, own, inner), F32),
-        pltpu.VMEM((own, inner), BF16),
         pltpu.VMEM((2, 256 + 16, inner), F32),
     ]
     slots = SIZES["c"] + SIZES["x"] * SIZES["y"] + SIZES["z"]
@@ -700,8 +696,8 @@
         pltpu.SemaphoreType.DMA((slots,)),
     ]
     shapes = (
-        jax.ShapeDtypeStruct((own, inner), BF16),
-        jax.ShapeDtypeStruct((9, 128), F32),
+        pltpu.VMEM((own, inner), BF16),
+        pltpu.VMEM((9, 128), F32),
     )
     alone = everyone is not None
 
@@ -728,7 +724,7 @@
         body,
         out_shape=shapes,
         in_specs=[hbm] * count + [VM] * alone,
-        out_specs=(hbm, VM),
+        out_specs=(VM, VM),
         scratch_shapes=([] if alone else remote) + stores + scratch,
         compiler_params=params,
         interpret=interpret,
@@ -736,12 +732,14 @@
     )(*inputs, *([everyone] if alone else []))
 
 
-def emit_kernel(enc_ref, pay_ref, out_ref, rate_ref, bias_ref, conv_ref):
+def emit_kernel(enc_ref, pay_ref, out_hbm, rate_ref, bias_ref, conv_ref, sem):
+    leave = pltpu.make_async_copy(enc_ref, out_hbm, sem)
+    leave.start()
     heads = rate_ref.shape[1]
-    out_ref[...] = enc_ref[...]
     rate_ref[...] = pay_ref[8:9, 0:heads]
     bias_ref[...] = pay_ref[8:9, heads : 2 * heads]
     conv_ref[...] = jnp.concatenate([pay_ref[0:4, :], pay_ref[4:8, :]], axis=1)
+    leave.wait()
 
 
 def emit(encoded, pay, heads):
@@ -754,9 +752,13 @@
             jax.ShapeDtypeStruct((4, 256), F32),
         ),
         in_specs=[VM] * 2,
-        out_specs=(VM,) * 4,
+        out_specs=(pl.BlockSpec(memory_space=pl.ANY), VM, VM, VM),
+        scratch_shapes=[pltpu.SemaphoreType.DMA],
         name="emit",
-    )(encoded, pay)
+    )(
+        pltpu.with_memory_space_constraint(encoded, pltpu.VMEM),
+        pltpu.with_memory_space_constraint(pay, pltpu.VMEM),
+    )
 
 
 def solution(mesh):

time: 38.7 us -> 37.7 us (0.974)
  Pallas kernels: 38 us -> 37 us
    pallas_call x1, Pallas kernels: 36.3 us -> 35.7 us  [layer(): pl.pallas_call(body, out_shape=shapes, in_specs=[hbm] * count + [VM] * al...]
where the time goes in v5:
time: 37.7 us; the launch traced here: 37.6 us
  Pallas kernels  37 us (98%)
  between operations  0.65 us (2%)
    pallas_call x1, Pallas kernels, layer(): pl.pallas_call(body, out_shape=shapes, in_specs=[hbm] * count + [VM] * al...  35.7 us
    pallas_call x1, Pallas kernels, emit(): pl.pallas_call(emit_kernel, out_shape=(jax.ShapeDtypeStruct(encoded.shape...  1.31 us

profile of v5, /device:TPU:1, one launch (start us, length us, event | category | flops | bytes accessed | tf_op | source)
XLA Modules:
  0.0 37.6 jit_solution(12414999907551000562)
XLA Ops:
  0.6 35.7 %layer.1 = (bf16[256,512]{1,0:T(8,128)(2,1)S(1)}, f32[9,128]{1,0:T(8,128)S(1)}) custom-call(s32[2,128]{1,0:T(2,128)} %bitcast.9, s32[4]{0:T(128)} %refs_1_.1, f32[4]{0:T(128)} %refs_2_.1, f32[4]{0:T(128)} %refs_3_.1, f32[4]{0:T(128)} %refs_4_.1, bf16[4,2048]{1,0:T(4,128)(2,1)} %refs_5_.1, f32[1,2048]{1,0:T(1,128)} %bitcast.7, f32[4,512]{1,0:T(4,128)} %refs_7_.1, ...), custom_call_target="tpu_custom_call" | custom-call | tf_op jit(solution)/shard_map/layer/pallas_call | solution.py:723
  36.3 1.3 %emit.1 = (bf16[256,512]{1,0:T(8,128)(2,1)}, f32[1,32]{1,0:T(1,128)}, f32[1,32]{1,0:T(1,128)}, f32[4,256]{1,0:T(4,128)}) custom-call(bf16[256,512]{1,0:T(8,128)(2,1)S(1)} %get-tuple-element.10.enc_ref, f32[9,128]{1,0:T(8,128)S(1)} %get-tuple-element.11.pay_ref), custom_call_target="tpu_custom_call" | custom-call | tf_op jit(solution)/shard_map/emit/pallas_call | solution.py:746

commit v6 on v5

--- a/solution.py
+++ b/solution.py
@@ -45,7 +45,22 @@
 
 
 def fold(v):
-    return v[:, :128] + v[:, 128:]
+    return v[:, :128] + v[:, 128:] if v.shape[1] > 128 else v
+
+
+def live(strand):
+    if strand == 0:
+        return ((slice(0, 128), slice(0, 128)), (slice(128, 256), slice(0, 256)))
+    return ((slice(0, 128), slice(0, 256)), (slice(128, 256), slice(128, 256)))
+
+
+def filled(halves, strand):
+    zero = jnp.zeros((128, 128), halves[0].dtype)
+    if strand == 0:
+        return jnp.concatenate(
+            [jnp.concatenate([halves[0], zero], axis=1), halves[1]], axis=0
+        )
+    return jnp.concatenate([halves[0], jnp.concatenate([zero, halves[1]], axis=1)], axis=0)
 
 
 def iota(shape, dim):
@@ -215,7 +230,7 @@
 
 
 def layer_kernel(
-    place, links, sources, enc_ref, pay_ref, held, stores, kmer_ref, last_ref, rows_ref, decay_ref, load_sem,
+    place, links, sources, enc_ref, rate_ref, bias_ref, conv_ref, held, stores, kmer_ref, last_ref, rows_ref, decay_ref, load_sem,
     xh_ref, xl_ref, y_ref, gate_ref, grow_ref, dg_ref, score_ref, gh_ref, gl_ref, car_ref, kxw_ref,
     *, loss_scale,
 ):
@@ -244,13 +259,13 @@
     normed = jnp.concatenate([normed, jnp.zeros((12, e.shape[1]), BF16)], axis=0)
     loads[10].wait()
     table_s = dot(normed, ws_ref[...])[0:4]
+    if links is not None:
+        links.met()
+        links.send_tokens(tok_ref)
     loads[11].wait()
     table_d = dot(normed, wst_ref[...], 1, 1)[0:4]
     loads[12].wait()
     table_v = dot(normed, wv_ref[...])[0:4]
-    if links is not None:
-        links.met()
-        links.send_tokens(tok_ref)
     loads[13].wait()
     table_z = dot(normed, wg_ref[...])[0:4]
     lane_h = iota((1, heads), 1)
@@ -337,18 +352,19 @@
     columns = jnp.transpose(
         jnp.concatenate([cum8, jnp.zeros((128 - 2 * heads, own), F32)], axis=0)
     )
+    square = (iota((128, 128), 0), iota((128, 128), 1))
+    causal = (square[0] >= square[1], square[0] <= square[1])
     for n in range(2 * heads):
-        if n < heads:
-            causal = iota((own, own), 0) >= iota((own, own), 1)
-        else:
-            causal = iota((own, own), 0) <= iota((own, own), 1)
         cum_c = jnp.broadcast_to(columns[:, n : n + 1], (own, 128))
-        for half in range(own // 128):
-            at = slice(half * 128, half * 128 + 128)
-            decay_ref[n, :, at] = (
-                jnp.where(causal[:, at], jnp.exp(cum_c - cum_rows[n][:, at]), 0.0)
-                * step_rows[n][:, at]
-            )
+        for rows, _ in live(n // heads):
+            for half in range(own // 128):
+                cols = slice(half * 128, half * 128 + 128)
+                if (cols.start > rows.start) if n < heads else (cols.start < rows.start):
+                    continue
+                grown = jnp.exp(cum_c[rows] - cum_rows[n][:, cols])
+                if cols.start == rows.start:
+                    grown = jnp.where(causal[n // heads], grown, 0.0)
+                decay_ref[n, rows, cols] = grown * step_rows[n][:, cols]
         part = slice((n % heads) * HEAD, (n % heads + 1) * HEAD)
         grow_ref[n // heads, :, part] = jnp.exp(cum_c)
     loads[14].wait()
@@ -399,7 +415,11 @@
             x_s = split(x_h)
             xh_ref[strand, :, part] = x_s[0]
             xl_ref[strand, :, part] = x_s[1]
-            mixing = split(scores * decay_ref[strand * heads + h])
+            mixing = [
+                split(scores[rows, cols] * decay_ref[strand * heads + h, rows, cols])
+                for rows, cols in live(strand)
+            ]
+            mixing = [filled([half[k] for half in mixing], strand) for k in range(2)]
             y_ref[strand, :, part] = dot(lhs3(mixing), rhs3(x_s)) + skip[h] * x_h
 
     if links is not None:
@@ -535,7 +555,7 @@
     rate_grads = [jnp.zeros((1, 128), F32)] * heads
     bias_grads = [jnp.zeros((1, 128), F32)] * heads
     tap_sums = [jnp.zeros((16, 2 * HEAD), F32)]
-    starts, d_scores, d_starts = [], [None, None], [None, None]
+    starts, d_scores, d_starts = [], [[None] * 2, [None] * 2], [None, None]
     for strand in range(2):
         kxw = kxw_parts[strand]
         start = dot(kb_t[0], kxw[0]) + (dot(kb_t[0], kxw[1]) + dot(kb_t[1], kxw[0]))
@@ -560,12 +580,25 @@
         d_y = d_normal - normal * jnp.mean(normal * d_normal, axis=1, keepdims=True)
         d_y = (d_y * inv) * gate
         x_s = (xh_ref[strand, :, part], xl_ref[strand, :, part])
-        mixed_grad = dot(lhs3(split(d_y)), rhs3(x_s, 1), 1, 1) * decay_ref[n]
-        d_scores[strand] = mixed_grad if h == 0 else d_scores[strand] + mixed_grad
-        weighted = mixed_grad * score_ref[strand]
-        wsum = split(fold(weighted) + d_y * from_start)
-        moved = dot(side, jnp.concatenate([wsum[0], wsum[1]], axis=0))
-        col_sum = jnp.sum(weighted, axis=0, keepdims=True)
+        mixed_grad = dot(lhs3(split(d_y)), rhs3(x_s, 1), 1, 1)
+        direct = d_y * from_start
+        wsum, col_sums = [], []
+        for half, (rows, cols) in enumerate(live(strand)):
+            grad = mixed_grad[rows, cols] * decay_ref[n, rows, cols]
+            d_scores[strand][half] = grad if h == 0 else d_scores[strand][half] + grad
+            weighted = grad * score_ref[strand, rows, cols]
+            wsum.append(split(fold(weighted) + direct[rows]))
+            col_sums.append(jnp.sum(weighted, axis=0, keepdims=True))
+        wsum = jnp.concatenate([wsum[0][0], wsum[1][0], wsum[0][1], wsum[1][1]], axis=0)
+        moved = dot(side, wsum)
+        if strand == 0:
+            col_sum = col_sums[1] + jnp.concatenate(
+                [col_sums[0], jnp.zeros((1, 128), F32)], axis=1
+            )
+        else:
+            col_sum = col_sums[0] + jnp.concatenate(
+                [jnp.zeros((1, 128), F32), col_sums[1]], axis=1
+            )
         grown = split(d_y * grow)
         gh_ref[strand, :, part] = grown[0]
         gl_ref[strand, :, part] = grown[1]
@@ -598,9 +631,10 @@
             bias_grads[h] = bias_grads[h] + slope[2 * heads + h : 2 * heads + h + 1, part]
 
     def local_pass(strand):
-        d_scores_s = split(d_scores[strand])
+        whole = filled(d_scores[strand], strand)
+        d_scores_s = split(whole)
         d_c = dot(lhs3(d_scores_s), rhs3(b_parts[strand])) + dot(lhs3((gh_ref[strand], gl_ref[strand])), rhs3(starts[strand], 1), 1, 1)
-        d_b = dot(lhs3(split(jnp.transpose(d_scores[strand]))), rhs3(c_parts[strand]))
+        d_b = dot(lhs3(split(jnp.transpose(whole))), rhs3(c_parts[strand]))
         d_sum = split(jnp.concatenate([d_b, d_c], axis=1) * slopes[strand])
         hits = hits_t[strand].astype(BF16)
         tap_sums[0] = tap_sums[0] + dot(
@@ -645,7 +679,9 @@
     value = jnp.concatenate([conv[:, :128], conv[:, 128:], last[0:1]], axis=0)
     if links is not None:
         value = links.reduce(value)
-    pay_ref[...] = value
+    rate_ref[...] = value[8:9, 0:head_total]
+    bias_ref[...] = value[8:9, head_total : 2 * head_total]
+    conv_ref[...] = jnp.concatenate([value[0:4], value[4:8]], axis=1)
     if links is not None:
         links.drain()
 
@@ -654,6 +690,7 @@
     (tokens, rc_map, embedding, norm_gain, w_values, w_gates, w_states, w_steps, conv_values,
      conv_states, step_bias, log_rate, skip_gain, head_gain, cotangent) = args
     own, inner = cotangent.shape
+    all_heads = 8 * step_bias.shape[0]
     blocks = SIZES["x"] * SIZES["z"]
     chunks = 2 * blocks
     hbm = pl.BlockSpec(memory_space=pl.ANY)
@@ -697,7 +734,9 @@
     ]
     shapes = (
         pltpu.VMEM((own, inner), BF16),
-        pltpu.VMEM((9, 128), F32),
+        pltpu.VMEM((1, all_heads), F32),
+        pltpu.VMEM((1, all_heads), F32),
+        pltpu.VMEM((4, 256), F32),
     )
     alone = everyone is not None
 
@@ -706,9 +745,9 @@
         sources, refs = refs[:count], refs[count:]
         if alone:
             links, held, refs = None, refs[0], refs[1:]
-            out, refs = refs[:2], refs[2:]
+            out, refs = refs[:4], refs[4:]
         else:
-            out, refs = refs[:2], refs[2:]
+            out, refs = refs[:4], refs[4:]
             links, held, refs = Links(refs[:8]), refs[0], refs[8:]
         layer_kernel(
             place, links, sources, *out, held, refs[:count], *refs[count:], loss_scale=loss_scale
@@ -724,7 +763,7 @@
         body,
         out_shape=shapes,
         in_specs=[hbm] * count + [VM] * alone,
-        out_specs=(VM, VM),
+        out_specs=(VM,) * 4,
         scratch_shapes=([] if alone else remote) + stores + scratch,
         compiler_params=params,
         interpret=interpret,
@@ -732,33 +771,27 @@
     )(*inputs, *([everyone] if alone else []))
 
 
-def emit_kernel(enc_ref, pay_ref, out_hbm, rate_ref, bias_ref, conv_ref, sem):
-    leave = pltpu.make_async_copy(enc_ref, out_hbm, sem)
-    leave.start()
-    heads = rate_ref.shape[1]
-    rate_ref[...] = pay_ref[8:9, 0:heads]
-    bias_ref[...] = pay_ref[8:9, heads : 2 * heads]
-    conv_ref[...] = jnp.concatenate([pay_ref[0:4, :], pay_ref[4:8, :]], axis=1)
-    leave.wait()
-
-
-def emit(encoded, pay, heads):
+def emit_kernel(*refs):
+    count = len(refs) // 2
+    copies = [
+        pltpu.make_async_copy(refs[n], refs[count + n], refs[-1].at[n]) for n in range(count)
+    ]
+    for copy in copies:
+        copy.start()
+    for copy in copies:
+        copy.wait()
+
+
+def emit(results):
+    hbm = pl.BlockSpec(memory_space=pl.ANY)
     return pl.pallas_call(
         emit_kernel,
-        out_shape=(
-            jax.ShapeDtypeStruct(encoded.shape, BF16),
-            jax.ShapeDtypeStruct((1, heads), F32),
-            jax.ShapeDtypeStruct((1, heads), F32),
-            jax.ShapeDtypeStruct((4, 256), F32),
-        ),
-        in_specs=[VM] * 2,
-        out_specs=(pl.BlockSpec(memory_space=pl.ANY), VM, VM, VM),
-        scratch_shapes=[pltpu.SemaphoreType.DMA],
+        out_shape=tuple(jax.ShapeDtypeStruct(r.shape, r.dtype) for r in results),
+        in_specs=[VM] * len(results),
+        out_specs=(hbm,) * len(results),
+        scratch_shapes=[pltpu.SemaphoreType.DMA((len(results),))],
         name="emit",
-    )(
-        pltpu.with_memory_space_constraint(encoded, pltpu.VMEM),
-        pltpu.with_memory_space_constraint(pay, pltpu.VMEM),
-    )
+    )(*[pltpu.with_memory_space_constraint(r, pltpu.VMEM) for r in results])
 
 
 def solution(mesh):
@@ -771,9 +804,8 @@
         def place():
             return lax.axis_index("ctx"), lax.axis_index("tp")
 
-        heads = args[11].shape[0] * mesh.shape["tp"]
-        encoded, pay = layer((args[0].reshape(2, 128),) + args[1:], place, loss_scale)
-        encoded, rate, bias, conv = emit(encoded, pay, heads)
+        results = layer((args[0].reshape(2, 128),) + args[1:], place, loss_scale)
+        encoded, rate, bias, conv = emit(results)
         return encoded, rate.reshape(-1), bias.reshape(-1), conv
 
     tp = P("tp")

time: 37.7 us -> 37.2 us (0.987)
  Pallas kernels: 37 us -> 36.4 us
    pallas_call x1, Pallas kernels: 1.31 us -> 0.75 us  [emit(): pl.pallas_call(emit_kernel, out_shape=tuple((jax.ShapeDtypeStruct(r.shape...]
where the time goes in v6:
time: 37.2 us; the launch traced here: 37.1 us
  Pallas kernels  36.4 us (98%)
  between operations  0.65 us (2%)
    pallas_call x1, Pallas kernels, layer(): pl.pallas_call(body, out_shape=shapes, in_specs=[hbm] * count + [VM] * al...  35.7 us
    pallas_call x1, Pallas kernels, emit(): pl.pallas_call(emit_kernel, out_shape=tuple((jax.ShapeDtypeStruct(r.shape...  0.75 us

profile of v6, /device:TPU:1, one launch (start us, length us, event | category | flops | bytes accessed | tf_op | source)
XLA Modules:
  0.0 37.1 jit_solution(3740128526204769274)
XLA Ops:
  0.6 35.7 %layer.1 = (bf16[256,512]{1,0:T(8,128)(2,1)S(1)}, f32[1,32]{1,0:T(1,128)S(1)}, f32[1,32]{1,0:T(1,128)S(1)}, f32[4,256]{1,0:T(4,128)S(1)}) custom-call(s32[2,128]{1,0:T(2,128)} %bitcast.9, s32[4]{0:T(128)} %refs_1_.1, f32[4]{0:T(128)} %refs_2_.1, f32[4]{0:T(128)} %refs_3_.1, f32[4]{0:T(128)} %refs_4_.1, bf16[4,2048]{1,0:T(4,128)(2,1)} %refs_5_.1, ...), custom_call_target="tpu_custom_call" | custom-call | tf_op jit(solution)/shard_map/layer/pallas_call | solution.py:762
  36.3 0.7 %emit.1 = (bf16[256,512]{1,0:T(8,128)(2,1)}, f32[1,32]{1,0:T(1,128)}, f32[1,32]{1,0:T(1,128)}, f32[4,256]{1,0:T(4,128)}) custom-call(bf16[256,512]{1,0:T(8,128)(2,1)S(1)} %get-tuple-element.12.refs_0_, f32[1,32]{1,0:T(1,128)S(1)} %get-tuple-element.13.refs_1_, f32[1,32]{1,0:T(1,128)S(1)} %get-tuple-element.14.refs_2_, f32[4,256]{1,0:T(4,128)S(1)} %get-tuple-element.15.refs_3_), custom_call_target="tpu_custom_call" | custom-call | tf_op jit(solution)/shard_map/emit/pallas_call | solution.py:787

commit v7 on v6

--- a/solution.py
+++ b/solution.py
@@ -136,7 +136,7 @@
         devices += [self.device(self.moved("x", step)) for step in offsets("x")]
         devices += [self.beside(1), self.beside(-1)]
         devices += [self.device(self.moved("xy", step)) for step in offsets("xy") if step[1]]
-        devices += [self.device(self.moved("c", step)) for step in offsets("c")]
+        devices += [self.device(self.moved("zc", step)) for step in offsets("zc") if step[1]]
         for device in devices:
             pl.semaphore_signal(barrier, inc=1, device_id=device, device_id_type=MESH)
         self.greeted = len(devices)
@@ -188,7 +188,7 @@
 
     def reduce(self, value):
         base = 0
-        for number, axes in enumerate(("c", "xy", "z")):
+        for number, axes in enumerate(("zc", "xy")):
             self.sent[number] = value
             steps = offsets(axes)
             sending = []
@@ -721,12 +721,12 @@
         pltpu.VMEM((2, own, inner), F32),
         pltpu.VMEM((2, 256 + 16, inner), F32),
     ]
-    slots = SIZES["c"] + SIZES["x"] * SIZES["y"] + SIZES["z"]
+    slots = SIZES["z"] * SIZES["c"] + SIZES["x"] * SIZES["y"]
     remote = [
         pltpu.VMEM((SIZES["z"], SIZES["x"], 2, 128), jnp.int32),
         pltpu.VMEM((2, 2, 128), jnp.int32),
         pltpu.VMEM((slots, 9, 128), F32),
-        pltpu.VMEM((3, 9, 128), F32),
+        pltpu.VMEM((2, 9, 128), F32),
         pltpu.SemaphoreType.DMA((12,)),
         pltpu.SemaphoreType.DMA((14,)),
         pltpu.SemaphoreType.DMA((slots,)),

time: 37.2 us -> 37.1 us (level)
  no operation moved by 1% of the time
where the time goes in v7:
time: 37.1 us
  Pallas kernels  36.4 us (98%)
  between operations  0.65 us (2%)
    pallas_call x1, Pallas kernels, layer(): pl.pallas_call(body, out_shape=shapes, in_specs=[hbm] * count + [VM] * al...  35.7 us
    pallas_call x1, Pallas kernels, emit(): pl.pallas_call(emit_kernel, out_shape=tuple((jax.ShapeDtypeStruct(r.shape...  0.75 us

profile of v7, /device:TPU:1, one launch (start us, length us, event | category | flops | bytes accessed | tf_op | source)
XLA Modules:
  0.0 37.1 jit_solution(10812989388208626026)
XLA Ops:
  0.6 35.7 %layer.1 = (bf16[256,512]{1,0:T(8,128)(2,1)S(1)}, f32[1,32]{1,0:T(1,128)S(1)}, f32[1,32]{1,0:T(1,128)S(1)}, f32[4,256]{1,0:T(4,128)S(1)}) custom-call(s32[2,128]{1,0:T(2,128)} %bitcast.9, s32[4]{0:T(128)} %refs_1_.1, f32[4]{0:T(128)} %refs_2_.1, f32[4]{0:T(128)} %refs_3_.1, f32[4]{0:T(128)} %refs_4_.1, bf16[4,2048]{1,0:T(4,128)(2,1)} %refs_5_.1, ...), custom_call_target="tpu_custom_call" | custom-call | tf_op jit(solution)/shard_map/layer/pallas_call | solution.py:762
  36.3 0.7 %emit.1 = (bf16[256,512]{1,0:T(8,128)(2,1)}, f32[1,32]{1,0:T(1,128)}, f32[1,32]{1,0:T(1,128)}, f32[4,256]{1,0:T(4,128)}) custom-call(bf16[256,512]{1,0:T(8,128)(2,1)S(1)} %get-tuple-element.12.refs_0_, f32[1,32]{1,0:T(1,128)S(1)} %get-tuple-element.13.refs_1_, f32[1,32]{1,0:T(1,128)S(1)} %get-tuple-element.14.refs_2_, f32[4,256]{1,0:T(4,128)S(1)} %get-tuple-element.15.refs_3_), custom_call_target="tpu_custom_call" | custom-call | tf_op jit(solution)/shard_map/emit/pallas_call | solution.py:787

commit v8 on v6

--- a/solution.py
+++ b/solution.py
@@ -487,8 +487,9 @@
             ids = jnp.broadcast_to(kmer_ref[chunk : chunk + 1, :], (64, 128)).astype(BF16)
             hits.append(jnp.where(ids == first_id, one16, zero16))
         found = dot(jnp.concatenate(hits, axis=1), jnp.concatenate(weights, axis=1), 1, 1)
-        acc_f = acc_f + jnp.where(block < me, found, 0.0)
-        acc_r = acc_r + jnp.where(block > me, found, 0.0)
+        acc_r = acc_r + found
+        acc_f = jnp.where(block == me, acc_r, acc_f)
+        acc_r = jnp.where(block == me, 0.0, acc_r)
     lane = iota((16, 128), 1)
     e_f = split(jnp.where(lane < CONV - 1, load_rows(0), 0.0))
     e_r = split(jnp.where(lane >= 128 - (CONV - 1), load_rows(chunks - 1), 0.0))
@@ -773,8 +774,12 @@
 
 def emit_kernel(*refs):
     count = len(refs) // 2
+    rows = refs[0].shape[0] // 4
+    pieces = [(refs[0].at[r : r + rows], refs[count].at[r : r + rows]) for r in range(0, 4 * rows, rows)]
+    pieces += [(refs[n], refs[count + n]) for n in range(1, count)]
     copies = [
-        pltpu.make_async_copy(refs[n], refs[count + n], refs[-1].at[n]) for n in range(count)
+        pltpu.make_async_copy(source, target, refs[-1].at[n])
+        for n, (source, target) in enumerate(pieces)
     ]
     for copy in copies:
         copy.start()
@@ -789,7 +794,7 @@
         out_shape=tuple(jax.ShapeDtypeStruct(r.shape, r.dtype) for r in results),
         in_specs=[VM] * len(results),
         out_specs=(hbm,) * len(results),
-        scratch_shapes=[pltpu.SemaphoreType.DMA((len(results),))],
+        scratch_shapes=[pltpu.SemaphoreType.DMA((len(results) + 3,))],
         name="emit",
     )(*[pltpu.with_memory_space_constraint(r, pltpu.VMEM) for r in results])
 

time: 37.2 us -> 37.2 us (level)
  no operation moved by 1% of the time
where the time goes in v8:
time: 37.2 us; the launch traced here: 37.1 us
  Pallas kernels  36.5 us (98%)
  between operations  0.65 us (2%)
    pallas_call x1, Pallas kernels, layer(): pl.pallas_call(body, out_shape=shapes, in_specs=[hbm] * count + [VM] * al...  35.7 us
    pallas_call x1, Pallas kernels, emit(): pl.pallas_call(emit_kernel, out_shape=tuple((jax.ShapeDtypeStruct(r.shape...  0.76 us

profile of v8, /device:TPU:1, one launch (start us, length us, event | category | flops | bytes accessed | tf_op | source)
XLA Modules:
  0.0 37.1 jit_solution(7486731759093459480)
XLA Ops:
  0.6 35.7 %layer.1 = (bf16[256,512]{1,0:T(8,128)(2,1)S(1)}, f32[1,32]{1,0:T(1,128)S(1)}, f32[1,32]{1,0:T(1,128)S(1)}, f32[4,256]{1,0:T(4,128)S(1)}) custom-call(s32[2,128]{1,0:T(2,128)} %bitcast.9, s32[4]{0:T(128)} %refs_1_.1, f32[4]{0:T(128)} %refs_2_.1, f32[4]{0:T(128)} %refs_3_.1, f32[4]{0:T(128)} %refs_4_.1, bf16[4,2048]{1,0:T(4,128)(2,1)} %refs_5_.1, ...), custom_call_target="tpu_custom_call" | custom-call | tf_op jit(solution)/shard_map/layer/pallas_call | solution.py:763
  36.3 0.8 %emit.1 = (bf16[256,512]{1,0:T(8,128)(2,1)}, f32[1,32]{1,0:T(1,128)}, f32[1,32]{1,0:T(1,128)}, f32[4,256]{1,0:T(4,128)}) custom-call(bf16[256,512]{1,0:T(8,128)(2,1)S(1)} %get-tuple-element.12.refs_0_, f32[1,32]{1,0:T(1,128)S(1)} %get-tuple-element.13.refs_1_, f32[1,32]{1,0:T(1,128)S(1)} %get-tuple-element.14.refs_2_, f32[4,256]{1,0:T(4,128)S(1)} %get-tuple-element.15.refs_3_), custom_call_target="tpu_custom_call" | custom-call | tf_op jit(solution)/shard_map/emit/pallas_call | solution.py:792

commit v9 on v8

--- a/solution.py
+++ b/solution.py
@@ -354,6 +354,8 @@
     )
     square = (iota((128, 128), 0), iota((128, 128), 1))
     causal = (square[0] >= square[1], square[0] <= square[1])
+    if links is not None:
+        links.pass_tokens(tok_ref)
     for n in range(2 * heads):
         cum_c = jnp.broadcast_to(columns[:, n : n + 1], (own, 128))
         for rows, _ in live(n // heads):
@@ -372,7 +374,6 @@
     dg_ref[...] = cot_ref[...].astype(F32) * (gain * loss_scale)
 
     if links is not None:
-        links.pass_tokens(tok_ref)
         links.take_beside(tok_ref)
         earlier, later = links.near[0], links.near[1]
     else:

time: 37.2 us -> 37.5 us (level)
  no operation moved by 1% of the time
where the time goes in v9:
time: 37.5 us; the launch traced here: 37.4 us
  Pallas kernels  36.8 us (98%)
  between operations  0.65 us (2%)
    pallas_call x1, Pallas kernels, layer(): pl.pallas_call(body, out_shape=shapes, in_specs=[hbm] * count + [VM] * al...  36 us
    pallas_call x1, Pallas kernels, emit(): pl.pallas_call(emit_kernel, out_shape=tuple((jax.ShapeDtypeStruct(r.shape...  0.76 us

profile of v9, /device:TPU:1, one launch (start us, length us, event | category | flops | bytes accessed | tf_op | source)
XLA Modules:
  0.0 37.4 jit_solution(7035045034205232927)
XLA Ops:
  0.6 36.0 %layer.1 = (bf16[256,512]{1,0:T(8,128)(2,1)S(1)}, f32[1,32]{1,0:T(1,128)S(1)}, f32[1,32]{1,0:T(1,128)S(1)}, f32[4,256]{1,0:T(4,128)S(1)}) custom-call(s32[2,128]{1,0:T(2,128)} %bitcast.9, s32[4]{0:T(128)} %refs_1_.1, f32[4]{0:T(128)} %refs_2_.1, f32[4]{0:T(128)} %refs_3_.1, f32[4]{0:T(128)} %refs_4_.1, bf16[4,2048]{1,0:T(4,128)(2,1)} %refs_5_.1, ...), custom_call_target="tpu_custom_call" | custom-call | tf_op jit(solution)/shard_map/layer/pallas_call | solution.py:764
  36.7 0.8 %emit.1 = (bf16[256,512]{1,0:T(8,128)(2,1)}, f32[1,32]{1,0:T(1,128)}, f32[1,32]{1,0:T(1,128)}, f32[4,256]{1,0:T(4,128)}) custom-call(bf16[256,512]{1,0:T(8,128)(2,1)S(1)} %get-tuple-element.12.refs_0_, f32[1,32]{1,0:T(1,128)S(1)} %get-tuple-element.13.refs_1_, f32[1,32]{1,0:T(1,128)S(1)} %get-tuple-element.14.refs_2_, f32[4,256]{1,0:T(4,128)S(1)} %get-tuple-element.15.refs_3_), custom_call_target="tpu_custom_call" | custom-call | tf_op jit(solution)/shard_map/emit/pallas_call | solution.py:793
